TPU v7x, 32 devices: a whole 2x2x4 slice. The times are simulated.
32 devices in a mesh: seq: 8 (over z, x), head: 4 (over y, core).
Axes of the slice: x: 2, y: 2, z: 4, core: 2. Of those that a mesh axis runs over, the one named last changes fastest.
Arguments:
- features: bfloat16 [8192, 8192], P(('seq', 'head')), may hold values from -6 to 6
- gate_input: bfloat16 [8192, 8192], P(('seq', 'head')), may hold values from -6 to 6
- bmat: bfloat16 [8192, 8, 128], P(('seq', 'head')), may hold values from -1.78125 to 1.78125
- cmat: bfloat16 [8192, 8, 128], P(('seq', 'head')), may hold values from -1.78125 to 1.78125
- step_size: float32 [8192, 128], P(('seq', 'head')), may hold values from 0.001 to 0.1
- log_decay: float32 [8192, 128], P(('seq', 'head')), may hold values from -0.8 to 0
- skip: float32 [128], P('head'), may hold values from 0.5 to 2
- norm_gain: float32 [8192], replicated, may hold values from 0.1 to 1.9
Outputs:
- mixed: bfloat16 [8192, 8192], P(('seq', 'head'))
All inputs are finite; a program needn't handle non-finite values.
Results may differ from a plain program's by a relative error of at most 0.0085.
Values may be sent and summed in bfloat16 or wider, within the bound.
No kernel may reach another device: no remote copies, remote signals or barrier semaphores. Data moves between devices by JAX's collectives and lax.ppermute only.
A program may use at most 128 MiB of HBM per device.

v0:
```python
import jax
import jax.numpy as jnp
import numpy as np
from jax import lax
from jax.experimental import pallas as pl
from jax.experimental.pallas import tpu as pltpu
from jax.sharding import PartitionSpec as P

SUB = 128
MID = SUB // 2 - 1
EXTRA = 8
PLANE = 4
AXES = ("seq", "head")
MIB = 2**20
F32, BF16 = jnp.float32, jnp.bfloat16
VM = pl.BlockSpec(memory_space=pltpu.VMEM)
SM = pl.BlockSpec(memory_space=pltpu.SMEM)
ANY = pl.BlockSpec(memory_space=pl.ANY)
CORE, CHIP, SIDE = 0, 1, 2


def split_two(value):
    high = value.astype(BF16)
    return high, (value - high.astype(F32)).astype(BF16)


def dot(a, b):
    return lax.dot_general(a, b, (((1,), (0,)), ((), ())), preferred_element_type=F32)


def dot_tn(a, b):
    return lax.dot_general(a, b, (((0,), (0,)), ((), ())), preferred_element_type=F32)


def dot_nt(a, b):
    return lax.dot_general(a, b, (((1,), (1,)), ((), ())), preferred_element_type=F32)


def spread_table(heads, groups, width):
    per_group = heads // groups
    row = np.arange(3 * heads - per_group)[:, None] % heads
    column = np.arange(width)[None, :] // (width // per_group)
    return jnp.asarray(row == heads - per_group + column, BF16)


def spread_of(table_ref, group, heads, groups):
    per_group = heads // groups
    start = pl.multiple_of(per_group * (groups - 1 - group), per_group)
    return table_ref[pl.ds(start, 2 * heads), :]


def pair_row(later, earlier, subs):
    return 1 + 2 * subs + later * (later - 1) // 2 + earlier


def decay_of(ref):
    rows = ref[-EXTRA:, :].astype(F32)
    return rows[0:1] + rows[1:2]


def put_decay(ref, decay):
    high, low = split_two(decay)
    row = lax.broadcasted_iota(jnp.int32, (EXTRA, decay.shape[1]), 0)
    both = jnp.where(row == 0, high.astype(F32), jnp.where(row == 1, low.astype(F32), 0.0))
    ref[-EXTRA:, :] = both.astype(BF16)


def write_scales(decay_ref, step_ref, sx_ref, sr_ref, sc_ref):
    rows, heads = decay_ref.shape
    subs = rows // SUB
    decay = decay_ref[...]
    high = decay.astype(BF16)
    rest = decay - high.astype(F32)
    mid = rest.astype(BF16)
    low = (rest - mid.astype(F32)).astype(BF16)
    row = lax.broadcasted_iota(jnp.int32, (rows, rows), 0)
    column = lax.broadcasted_iota(jnp.int32, (rows, rows), 1)
    lower = (row >= column).astype(BF16)
    cum = dot(lower, high) + dot(lower, mid) + dot(lower, low)
    centre = [cum[b * SUB + MID : b * SUB + MID + 1] for b in range(subs)]
    last = cum[rows - 1 : rows]
    for b in range(subs):
        part = slice(b * SUB, (b + 1) * SUB)
        off = cum[part] - centre[b]
        high, low = split_two(jnp.exp(-off) * step_ref[part, :])
        sx_ref[part, :heads] = high
        sx_ref[part, heads:] = low
        high, low = split_two(jnp.exp(off))
        sr_ref[part, :heads] = high
        sr_ref[part, heads:] = low
    scalars = [last] + [last - c for c in centre] + centre
    for b in range(subs):
        scalars += [centre[b] - centre[a] for a in range(b)]
    pad = jnp.zeros((EXTRA - len(scalars), heads), F32)
    high, low = split_two(jnp.exp(jnp.concatenate(scalars + [pad], axis=0)))
    sc_ref[:, :heads] = high
    sc_ref[:, heads:] = low


def scaled_features(x_ref, sx_ref, spread):
    return (x_ref[...].astype(F32) * dot(sx_ref[...], spread)).astype(BF16)


def update_of(xa, b_group, scalars):
    total = None
    for b in range(xa.shape[0] // SUB):
        part = slice(b * SUB, (b + 1) * SUB)
        term = dot_tn(b_group[part], xa[part]) * scalars[1 + b : 2 + b]
        total = term if total is None else total + term
    return total


def own_update(group, x_ref, bg_ref, sx_ref, sc_ref, table_ref):
    groups = bg_ref.shape[0]
    spread = spread_of(table_ref, group, sx_ref.shape[1] // 2, groups)
    scalars = dot(sc_ref[...], spread)
    return update_of(scaled_features(x_ref, sx_ref, spread), bg_ref[group], scalars), scalars[0:1]


def away_group(ids, slot, groups):
    return (1 - ids[CORE]) * (groups // 2) + (ids[CHIP] ^ slot)


def home_group(ids, slot, groups):
    return ids[CORE] * (groups // 2) + (ids[CHIP] ^ slot)


def put_update(ref, update, decay):
    ref[:-EXTRA, :] = update.astype(BF16)
    put_decay(ref, decay)


def first_kernel(
    ids, x_ref, b_ref, step_ref, decay_ref, table_ref, u_ref, bg_ref, sx_ref, sr_ref, sc_ref, b32
):
    i = pl.program_id(0)
    rows, groups, state = b_ref.shape

    @pl.when(i == 0)
    def _():
        write_scales(decay_ref, step_ref, sx_ref, sr_ref, sc_ref)
        b32[...] = b_ref[...].astype(F32).reshape(rows * groups, state)
        for g in range(groups):
            bg_ref[g] = b32[pl.ds(g, rows, stride=groups), :].astype(BF16)

    group = away_group(ids, 3 - i, groups)
    put_update(u_ref.at[0], *own_update(group, x_ref, bg_ref, sx_ref, sc_ref, table_ref))


def second_kernel(ids, x_ref, bg_ref, sx_ref, sc_ref, table_ref, u_ref):
    group = away_group(ids, 1 - pl.program_id(0), bg_ref.shape[0])
    put_update(u_ref.at[0], *own_update(group, x_ref, bg_ref, sx_ref, sc_ref, table_ref))


def home_kernel(slot, ids, x_ref, bg_ref, sx_ref, sc_ref, table_ref, far_ref, u_ref, p0, p1):
    i = pl.program_id(0)
    group = home_group(ids, slot - i, bg_ref.shape[0])
    update, decay = own_update(group, x_ref, bg_ref, sx_ref, sc_ref, table_ref)
    put_update(u_ref.at[0], update, decay)
    far, far_decay = far_ref[0, :-EXTRA, :].astype(F32), decay_of(far_ref.at[0])
    late = ids[CORE].astype(F32)
    joined = update * (late + (1.0 - late) * far_decay) + far * ((1.0 - late) + late * decay)
    both = decay * far_decay
    pl.when(i == 0)(lambda: put_update(p0, joined, both))
    pl.when(i == 1)(lambda: put_update(p1, joined, both))


def skip_kernel(ids, *refs):
    pieces, out_ref = refs[:-2], refs[-1]
    groups, _, width = out_ref.shape
    share = pieces[0].shape[1]
    heads = share * len(pieces)
    own = 2 * ids[CHIP] + ids[CORE]
    place = own & (len(pieces) - 1)
    row = lax.broadcasted_iota(jnp.int32, (share, width), 0)
    column = lax.broadcasted_iota(jnp.int32, (share, width), 1) // (width * groups // heads)
    spread_groups = share * groups // heads
    for m, piece in enumerate(pieces):
        high, low = split_two(jnp.broadcast_to(piece[...], (EXTRA, share)))
        for k in range(spread_groups):
            pick = (row == column + k * (heads // groups)).astype(BF16)
            out_ref[(place ^ m) * spread_groups + k] = dot(high, pick) + dot(low, pick)


def gate_kernel(gate_ref, out_ref):
    half = 0.5 * gate_ref[...].astype(F32)
    out_ref[0] = half + half * jnp.tanh(half)


def local_kernel(
    ids, x_ref, c_ref, bg_ref, sx_ref, sr_ref, sc_ref, table_ref, y_ref, r_ref, cg_ref, c32
):
    i = pl.program_id(0)
    group = i
    rows, groups, state = c_ref.shape
    heads = sx_ref.shape[1] // 2
    subs = rows // SUB

    @pl.when(i == 0)
    def _():
        c32[...] = c_ref[...].astype(F32).reshape(rows * groups, state)

    c_group = c32[pl.ds(group, rows, stride=groups), :].astype(BF16)
    cg_ref[0] = c_group
    spread = spread_of(table_ref, group, heads, groups)
    scalars = dot(sc_ref[...], spread)
    xa = scaled_features(x_ref, sx_ref, spread)
    row_scale = dot(sr_ref[...], spread)
    row = lax.broadcasted_iota(jnp.int32, (SUB, SUB), 0)
    column = lax.broadcasted_iota(jnp.int32, (SUB, SUB), 1)
    b_group = bg_ref[group]
    for b in range(subs):
        part = slice(b * SUB, (b + 1) * SUB)
        scores = jnp.where(row >= column, dot_nt(c_group[part], b_group[part]), 0.0)
        inner = dot(scores.astype(BF16), xa[part])
        for a in range(b):
            other = slice(a * SUB, (a + 1) * SUB)
            scores = dot_nt(c_group[part], b_group[other]).astype(BF16)
            at = pair_row(b, a, subs)
            inner = inner + dot(scores, xa[other]) * scalars[at : at + 1]
        y_ref[0, part, :] = row_scale[part] * inner
        r_ref[0, part, :] = row_scale[part] * scalars[1 + subs + b : 2 + subs + b]


def hold(held, place, pieces):
    for m, piece in enumerate(pieces):
        held[place ^ m] = piece[...]


def fold(held):
    total, decay = held[0, :-EXTRA, :].astype(F32), decay_of(held.at[0])
    for k in range(1, PLANE):
        d = decay_of(held.at[k])
        total = d * total + held[k, :-EXTRA, :].astype(F32)
        decay = d * decay
    return total, decay


def plane_down_kernel(ids, p0, p1, p2, p3, *refs):
    o0, o1, o2, o3, held, cut = refs[-6:]
    hold(held, ids[CHIP], (p0, p1, p2, p3))
    total, decay = fold(held)
    quarter = total.shape[1] // PLANE
    for k in range(PLANE):
        part = slice(k * quarter, (k + 1) * quarter)
        put_update(cut.at[k], total[:, part], decay[:, part])
    for m, out in enumerate((o0, o1, o2, o3)):
        out[...] = cut[ids[SIDE] ^ m]


def side_total_kernel(ids, p0, p1, p2, p3, out_ref, held):
    hold(held, ids[SIDE], (p0, p1, p2, p3))
    put_update(out_ref, *fold(held))


def side_up_kernel(ids, p0, p1, p2, p3, *refs):
    o0, o1, o2, o3, held, state = refs[-6:]
    hold(held, ids[SIDE], (p0, p1, p2, p3))
    if len(refs) == 8:
        state[0] = refs[0][:-EXTRA, :]
    else:
        state[0] = jnp.zeros(state.shape[1:], BF16)
    states_after(held, state)
    for m, out in enumerate((o0, o1, o2, o3)):
        out[...] = state[ids[SIDE] ^ m]


def states_after(held, state):
    now = state[0].astype(F32)
    for k in range(1, PLANE):
        now = decay_of(held.at[k - 1]) * now + held[k - 1, :-EXTRA, :].astype(F32)
        state[k] = now.astype(BF16)


def plane_up_kernel(ids, e0, e1, e2, e3, p0, p1, p2, p3, *refs):
    o0, o1, o2, o3, held, state, enter = refs[-7:]
    quarter = e0.shape[1]
    hold(held, ids[CHIP], (p0, p1, p2, p3))
    for m, piece in enumerate((e0, e1, e2, e3)):
        enter[ids[SIDE] ^ m] = piece[...]
    for k in range(PLANE):
        state[0, :, k * quarter : (k + 1) * quarter] = enter[k]
    states_after(held, state)
    for m, out in enumerate((o0, o1, o2, o3)):
        out[...] = state[ids[CHIP] ^ m]


def small_call(kernel, ids, args, outs, scratch=(), after=()):
    size = sum(a.size * 2 for a in args) + sum(2 * o.size for o in outs)
    return pl.pallas_call(
        kernel,
        out_shape=outs,
        in_specs=[SM] + [VM] * len(args) + [ANY] * len(after),
        out_specs=[VM] * len(outs),
        scratch_shapes=list(scratch),
        compiler_params=pltpu.CompilerParams(vmem_limit_bytes=8 * MIB),
        cost_estimate=pl.CostEstimate(flops=size, bytes_accessed=size, transcendentals=0),
    )(ids, *args, *after)


def exchange(value, mask, count):
    return lax.ppermute(value, AXES, [(i, i ^ mask) for i in range(count)])


def exchange_pieces(pieces, mask, count):
    moved = {}
    for m in (3, 2, 1):
        moved[m] = exchange(pieces[m], mask * m, count)
    return [pieces[0], moved[1], moved[2], moved[3]]


def shifted(value, steps, count):
    return lax.ppermute(value, AXES, [(i, i + steps) for i in range(count - steps)])


def scan_groups(total, stride, count):
    places = count // stride

    def parts(message):
        decay = message[-EXTRA].astype(F32) + message[-EXTRA + 1].astype(F32)
        return message[:-EXTRA].astype(F32), decay

    def packed(value, decay):
        high, low = split_two(decay)
        rest = jnp.zeros((EXTRA - 2, decay.shape[0]), BF16)
        return jnp.concatenate([value.astype(BF16), high[None], low[None], rest], axis=0)

    covered = shifted(total, stride, count)
    reach = 1
    while reach < places - 1:
        value, decay = parts(covered)
        own, own_decay = parts(total)
        longer = packed(own_decay[None] * value + own, own_decay * decay)
        far, far_decay = parts(shifted(longer, stride * (reach + 1), count))
        covered = packed(decay[None] * far + value, decay * far_decay)
        reach = 2 * reach + 1
    return covered


def finish_kernel(entries, ids, x_ref, y_ref, r_ref, gate_ref, cg_ref, gain_ref, skip_ref, *refs):
    count = len(entries)
    states, updates = refs[:count], refs[count : 2 * count]
    out_ref, held, made, sems = refs[-4:]
    groups, rows, width = y_ref.shape
    copies = []
    for n, (slot, side, at) in enumerate(entries):
        group = (ids[CORE] ^ side) * (groups // 2) + (ids[CHIP] ^ slot)

        @pl.when(ids[CORE] == 0)
        def _():
            held[n] = states[n][...]

        @pl.when(ids[CORE] == 1)
        def _():
            after = decay_of(updates[n].at[at]) * states[n][...].astype(F32)
            held[n] = (after + updates[n][at, :-EXTRA, :].astype(F32)).astype(BF16)

        columns = pl.ds(pl.multiple_of(group * width, width), width)
        gain, skip = gain_ref[:, columns], skip_ref[group, 0:1, :]
        for b in range(rows // SUB):
            part = slice(b * SUB, (b + 1) * SUB)
            carried = dot(cg_ref[group, part, :], held[n])
            ssm = y_ref[group, part, :] + r_ref[group, part, :] * carried
            ssm = (ssm + skip * x_ref[part, columns].astype(F32)).astype(BF16)
            gated = ssm.astype(F32) * gate_ref[group, part, :]
            mean = jnp.mean(gated * gated, axis=1, keepdims=True)
            made[n, part, :] = (gated * lax.rsqrt(mean + 1e-05) * gain).astype(BF16)
            copies.append(
                pltpu.make_async_copy(
                    made.at[n, part, :], out_ref.at[part, columns], sems.at[n, b]
                )
            )
            copies[-1].start()
    for copy in copies:
        copy.wait()


def shards(features, gate_input, bmat, cmat, step_size, log_decay, skip, norm_gain):
    rows, inner = features.shape
    groups, state = bmat.shape[1:]
    heads = step_size.shape[1]
    width = inner // groups
    count = lax.axis_size("seq") * lax.axis_size("head")
    me = lax.axis_index("seq") * lax.axis_size("head") + lax.axis_index("head")
    ids = jnp.stack([me & 1, (me >> 1) & (PLANE - 1), (me >> 3) & (PLANE - 1)]).astype(jnp.int32)
    tall = state + EXTRA
    table = spread_table(heads, groups, width)

    def far_memory(*values):
        return tuple(pltpu.with_memory_space_constraint(v, pltpu.HBM) for v in values)


    def out(*shape, kind=BF16):
        return jax.ShapeDtypeStruct(shape, kind)

    def whole(*shape):
        return pl.BlockSpec(shape, lambda i, *_: (0,) * len(shape))

    def block(place):
        return pl.BlockSpec((rows, width), lambda i, ids: (0, place(ids, i)))

    def call(kernel, steps, in_specs, out_specs, outs, args, scratch=(), aliases=None, cost=1, grant=8):
        return pl.pallas_call(
            kernel,
            grid_spec=pltpu.PrefetchScalarGridSpec(
                num_scalar_prefetch=1,
                grid=(steps,),
                in_specs=in_specs,
                out_specs=out_specs,
                scratch_shapes=list(scratch),
            ),
            out_shape=outs,
            input_output_aliases=aliases or {},
            compiler_params=pltpu.CompilerParams(vmem_limit_bytes=grant * MIB),
            cost_estimate=pl.CostEstimate(
                flops=cost * 10**9, bytes_accessed=cost * 4 * 2**20, transcendentals=0
            ),
        )(ids, *args)

    slot_spec = pl.BlockSpec((1, tall, width), lambda i, *_: (i, 0, 0))
    sx_spec, sc_spec = whole(rows, 2 * heads), whole(EXTRA, 2 * heads)
    table_spec, bg_spec = whole(*table.shape), whole(groups, rows, state)
    chunk = out(2, tall, width)

    away32, bg, sx, sr, sc = call(
        first_kernel,
        2,
        [
            block(lambda ids, i: away_group(ids, 3 - i, groups)),
            whole(rows, groups, state),
            whole(rows, heads),
            whole(rows, heads),
            table_spec,
        ],
        [slot_spec, bg_spec, sx_spec, sx_spec, sc_spec],
        [chunk, out(groups, rows, state), *[out(rows, 2 * heads)] * 2, out(EXTRA, 2 * heads)],
        far_memory(features, bmat, step_size, log_decay, table),
        [pltpu.VMEM((rows * groups, state), F32)],
    )
    far32 = exchange(away32, 1, count)
    (away10,) = call(
        second_kernel,
        2,
        [
            block(lambda ids, i: away_group(ids, 1 - i, groups)),
            bg_spec,
            sx_spec,
            sc_spec,
            table_spec,
        ],
        [slot_spec],
        [chunk],
        (features, bg, sx, sc, table),
    )
    far10 = exchange(away10, 1, count)

    def home(slot, far, earlier):
        def kernel(ids, *refs):
            home_kernel(slot, ids, *refs[:6], *refs[6 + len(earlier) :])

        half_spec = pl.BlockSpec((1, tall, width), lambda i, ids: (3 - slot + i, 0, 0))

        return call(
            kernel,
            2,
            [
                block(lambda ids, i: home_group(ids, slot - i, groups)),
                bg_spec,
                sx_spec,
                sc_spec,
                table_spec,
                slot_spec,
            ]
            + [ANY] * len(earlier),
            [half_spec, whole(tall, width), whole(tall, width)],
            [out(PLANE, tall, width), out(tall, width), out(tall, width)],
            (features, bg, sx, sc, table, far, *earlier),
            aliases={7: 0} if earlier else {},
        )

    own, piece3, piece2 = home(3, far32, ())
    moved3 = exchange(piece3, 6, count)
    moved2 = exchange(piece2, 4, count)
    own, piece1, piece0 = home(1, far10, (own,))
    pieces = [piece0, exchange(piece1, 2, count), moved2, moved3]

    group_block = pl.BlockSpec((1, rows, width), lambda i, ids: (i, 0, 0))
    y, r, cg = call(
        local_kernel,
        groups,
        [block(lambda ids, i: i), whole(rows, groups, state), bg_spec]
        + [sx_spec, sx_spec, sc_spec, table_spec],
        [group_block, group_block, pl.BlockSpec((1, rows, state), lambda i, ids: (i, 0, 0))],
        [out(groups, rows, width, kind=F32)] * 2 + [out(groups, rows, state)],
        (features, cmat, bg, sx, sr, sc, table),
        [pltpu.VMEM((rows * groups, state), F32)],
        cost=4,
        grant=14,
    )

    def gate(slot, earlier, after):
        def place(ids, i):
            return (ids[CORE] ^ (i & 1)) * (groups // 2) + (ids[CHIP] ^ (slot + i // 2))

        return call(
            lambda ids, gate_ref, *refs: gate_kernel(gate_ref, refs[-1]),
            4,
            [block(place)] + [ANY] * (len(earlier) + 1),
            [pl.BlockSpec((1, rows, width), lambda i, ids: (place(ids, i), 0, 0))],
            [out(groups, rows, width, kind=F32)],
            (*far_memory(gate_input), *earlier, after),
            aliases={2: 0} if earlier else {},
        )

    quarters = small_call(
        plane_down_kernel,
        ids,
        pieces,
        [out(tall, width // PLANE)] * PLANE,
        [pltpu.VMEM((PLANE, tall, width), BF16), pltpu.VMEM((PLANE, tall, width // PLANE), BF16)],
        [y],
    )
    sides = exchange_pieces(quarters, 8, count)
    skip, _ = lax.optimization_barrier((skip, quarters[0]))
    skips = [skip]
    for m in range(1, heads // skip.shape[0]):
        skips.append(exchange(skip, m, count))
    skips = [v.reshape(1, v.shape[0]) for v in skips]
    lacking, _ = lax.optimization_barrier((own, quarters[0]))
    lacking = lax.ppermute(lacking, AXES, [(i, i + 1) for i in range(0, count, 2)])
    side_scratch = [
        pltpu.VMEM((PLANE, tall, width // PLANE), BF16),
        pltpu.VMEM((PLANE, state, width // PLANE), BF16),
    ]
    enter = []
    stride = 2 * PLANE * PLANE
    if count > stride:
        (total,) = small_call(
            side_total_kernel, ids, sides, [out(tall, width // PLANE)], side_scratch[:1]
        )
        enter = [scan_groups(total, stride, count)]
    entering = small_call(
        side_up_kernel,
        ids,
        [*sides, *enter],
        [out(state, width // PLANE)] * PLANE,
        side_scratch,
    )
    gates = gate(0, (), entering[0])
    entering = exchange_pieces(entering, 8, count)
    states = small_call(
        plane_up_kernel,
        ids,
        (*entering, *pieces),
        [out(state, width)] * PLANE,
        [
            pltpu.VMEM((PLANE, tall, width), BF16),
            pltpu.VMEM((PLANE, state, width), BF16),
            pltpu.VMEM((PLANE, state, width // PLANE), BF16),
        ],
        [*gates, lacking],
    )
    states = exchange_pieces(states, 2, count)
    (skip_rows,) = small_call(
        skip_kernel, ids, skips, [out(groups, EXTRA, width, kind=F32)], (), [states[0]]
    )
    gain = norm_gain.reshape(1, inner)
    forwarded = []
    for s in states:
        forwarded.append(exchange(s, 1, count))

    def finish(entries, result):
        def kernel(*refs):
            finish_kernel([(m, side, (3 - m) % (4 if side else 2)) for m, side in entries], *refs)

        given = [forwarded[m] if side else states[m] for m, side in entries]
        updates = [lacking if side else far32 if m > 1 else far10 for m, side in entries]
        earlier = [] if result is None else [result]
        args = (ids, features, y, r, gates, cg, gain, skip_rows, *given, *updates)
        return pl.pallas_call(
            kernel,
            out_shape=out(rows, inner),
            in_specs=[SM] + [VM] * (len(args) - 1) + [ANY] * len(earlier),
            out_specs=ANY,
            scratch_shapes=[
                pltpu.VMEM((len(entries), state, width), BF16),
                pltpu.VMEM((len(entries), rows, width), BF16),
                pltpu.SemaphoreType.DMA((len(entries), rows // SUB)),
            ],
            input_output_aliases={len(args): 0} if earlier else {},
            compiler_params=pltpu.CompilerParams(vmem_limit_bytes=12 * MIB),
            cost_estimate=pl.CostEstimate(flops=10**9, bytes_accessed=4 * 2**20, transcendentals=0),
        )(*args, *earlier)

    (gates,) = gate(2, gates, states[0])
    result = finish([(0, 0), (0, 1)], None)
    result = finish([(3, 0)], result)
    result = finish([(2, 0), (1, 0), (3, 1), (2, 1)], result)
    return finish([(1, 1)], result)


def solution(mesh):
    return jax.shard_map(
        shards,
        mesh=mesh,
        in_specs=(
            P(("seq", "head"), None),
            P(("seq", "head"), None),
            P(("seq", "head"), None, None),
            P(("seq", "head"), None, None),
            P(("seq", "head"), None),
            P(("seq", "head"), None),
            P("head"),
            P(),
        ),
        out_specs=P(("seq", "head"), None),
        check_vma=False,
    )
```

profile of v0, /device:TPU:1, one launch (start us, length us, event | category | flops | bytes accessed | tf_op | source)
XLA Modules:
  0.0 81.0 jit_solution(5826167882980329271)
XLA Ops:
  0.0 0.1 pad_add_fusion.ids.refs_0_
  0.1 4.2 %shard_map.91 = (bf16[2,136,1024]{2,1,0:T(8,128)(2,1)S(1)}, bf16[8,256,128]{2,1,0:T(8,128)(2,1)S(1)}, bf16[256,256]{1,0:T(8,128)(2,1)S(1)}, bf16[256,256]{1,0:T(8,128)(2,1)S(1)}, bf16[8,256]{1,0:T(8,128)(2,1)S(1)}) custom-call(s32[3]{0:T(128)S(1)} %pad_add_fusion.ids.refs_0_, bf16[256,8192]{1,0:T(8,128)(2,1)} %refs_1_.7, bf16[256,8,128]{2,1,0:T(8,128)(2,1)} %b_ref.1, ...), custom_call_target="tpu_custom_call" | custom-call | flops 1000000000 | bytes 4194304 | tf_op jit(solution)/shard_map/pallas_call | solution.py:403
  4.3 0.1 collective-permute-start.1
  4.4 1.9 %shard_map.93 = bf16[2,136,1024]{2,1,0:T(8,128)(2,1)S(1)} custom-call(s32[3]{0:T(128)S(1)} %pad_add_fusion.ids.refs_0_, bf16[256,8192]{1,0:T(8,128)(2,1)S(1)} %copy-done, bf16[8,256,128]{2,1,0:T(8,128)(2,1)S(1)} %get-tuple-element.33.bg_ref.refs_1_, bf16[256,256]{1,0:T(8,128)(2,1)S(1)} %get-tuple-element.34.sx_ref.refs_2_, ...), custom_call_target="tpu_custom_call" | custom-call | flops 1000000000 | bytes 4194304 | tf_op jit(solution)/shard_map/pallas_call | solution.py:403
  6.2 0.5 collective-permute-start
  6.8 0.0 collective-permute-done.1.refs_5_.refs_9_.refs_12_
  6.8 2.0 %shard_map.94 = (bf16[4,136,1024]{2,1,0:T(8,128)(2,1)S(1)}, bf16[136,1024]{1,0:T(8,128)(2,1)S(1)}, bf16[136,1024]{1,0:T(8,128)(2,1)S(1)}) custom-call(s32[3]{0:T(128)S(1)} %pad_add_fusion.ids.refs_0_, bf16[256,8192]{1,0:T(8,128)(2,1)S(1)} %copy-done, bf16[8,256,128]{2,1,0:T(8,128)(2,1)S(1)} %get-tuple-element.33.bg_ref.refs_1_, ...), custom_call_target="tpu_custom_call" | custom-call | flops 1000000000 | bytes 4194304 | tf_op jit(solution)/shard_map/pallas_call | solution.py:403
  8.8 0.0 copy-start.4
  8.8 2.0 %shard_map.95 = (bf16[4,136,1024]{2,1,0:T(8,128)(2,1)S(1)}, bf16[136,1024]{1,0:T(8,128)(2,1)S(1)}, bf16[136,1024]{1,0:T(8,128)(2,1)S(1)}) custom-call(s32[3]{0:T(128)S(1)} %pad_add_fusion.ids.refs_0_, bf16[256,8192]{1,0:T(8,128)(2,1)S(1)} %copy-done, bf16[8,256,128]{2,1,0:T(8,128)(2,1)S(1)} %get-tuple-element.33.bg_ref.refs_1_, ...), custom_call_target="tpu_custom_call", output_to_operand_aliasing={{0}: (7, {})} | custom-call | flops 1000000000 | bytes 4194304 | tf_op jit(solution)/shard_map/pallas_call | solution.py:403
  10.9 2.3 %collective-permute-start.2 = (bf16[136,1024]{1,0:T(8,128)(2,1)S(1)}, bf16[136,1024]{1,0:T(8,128)(2,1)S(1)}, u32[]{:S(2)}, u32[]{:S(2)}) collective-permute-start(bf16[136,1024]{1,0:T(8,128)(2,1)S(1)} %get-tuple-element.42), channel_id=1, source_target_pairs={{0,2},{1,3},{2,0},{3,1},{4,6},{5,7},{6,4},{7,5},{8,10},{9,11},{10,... | collective-permute-start | bytes 835592 | tf_op jit(solution)/shard_map/ppermute | solution.py:302
  13.2 1.2 %collective-permute-start.3 = (bf16[136,1024]{1,0:T(8,128)(2,1)S(1)}, bf16[136,1024]{1,0:T(8,128)(2,1)S(1)}, u32[]{:S(2)}, u32[]{:S(2)}) collective-permute-start(bf16[136,1024]{1,0:T(8,128)(2,1)S(1)} %get-tuple-element.43), channel_id=1, source_target_pairs={{0,4},{1,5},{2,6},{3,7},{4,0},{5,1},{6,2},{7,3},{8,12},{9,13},{10,... | collective-permute-start | bytes 835592 | tf_op jit(solution)/shard_map/ppermute | solution.py:302
  14.4 0.1 collective-permute-start.4
  14.5 9.0 %shard_map.92 = (f32[8,256,1024]{2,1,0:T(8,128)S(1)}, f32[8,256,1024]{2,1,0:T(8,128)S(1)}, bf16[8,256,128]{2,1,0:T(8,128)(2,1)S(1)}) custom-call(s32[3]{0:T(128)S(1)} %pad_add_fusion.ids.refs_0_, bf16[256,8192]{1,0:T(8,128)(2,1)S(1)} %copy-done, bf16[256,8,128]{2,1,0:T(8,128)(2,1)S(1)} %copy-done.4, ...), custom_call_target="tpu_custom_call" | custom-call | flops 4000000000 | bytes 16777216 | tf_op jit(solution)/shard_map/pallas_call | solution.py:403
  23.5 0.0 collective-permute-done.2.p1
  23.5 3.2 %collective-permute-done.4.p3 = bf16[136,1024]{1,0:T(8,128)(2,1)S(1)} collective-permute-done((bf16[136,1024]{1,0:T(8,128)(2,1)S(1)}, bf16[136,1024]{1,0:T(8,128)(2,1)S(1)}, u32[]{:S(2)}, u32[]{:S(2)}) %collective-permute-start.4) | collective-permute-done | bytes 278560 | tf_op jit(solution)/shard_map/ppermute | solution.py:302
  26.7 1.0 %shard_map.96 = (bf16[136,256]{1,0:T(8,128)(2,1)S(1)}, bf16[136,256]{1,0:T(8,128)(2,1)S(1)}, bf16[136,256]{1,0:T(8,128)(2,1)S(1)}, bf16[136,256]{1,0:T(8,128)(2,1)S(1)}) custom-call(s32[3]{0:T(128)S(1)} %pad_add_fusion.ids.refs_0_, bf16[136,1024]{1,0:T(8,128)(2,1)S(1)} %get-tuple-element.41.p0, bf16[136,1024]{1,0:T(8,128)(2,1)S(1)} %collective-permute-done.2.p1, ...), custom_call_target="tpu_custom_call" | custom-call | flops 1392640 | bytes 1392640 | tf_op jit(solution)/shard_map/pallas_call | solution.py:290
  27.7 1.3 %collective-permute-start.11 = (bf16[4,136,1024]{2,1,0:T(8,128)(2,1)S(1)}, bf16[4,136,1024]{2,1,0:T(8,128)(2,1)S(1)}, u32[]{:S(2)}, u32[]{:S(2)}) collective-permute-start(bf16[4,136,1024]{2,1,0:T(8,128)(2,1)S(1)} %get-tuple-element.54), channel_id=1, source_target_pairs={{0,1},{2,3},{4,5},{6,7},{8,9},{10,11},{12,13},{14,15},{16,17},{18,... | collective-permute-start | bytes 3342344 | tf_op jit(solution)/shard_map/ppermute | solution.py:530
  29.0 1.2 %collective-permute-start.5 = (bf16[136,256]{1,0:T(8,128)(2,1)S(1)}, bf16[136,256]{1,0:T(8,128)(2,1)S(1)}, u32[]{:S(2)}, u32[]{:S(2)}) collective-permute-start(bf16[136,256]{1,0:T(8,128)(2,1)S(1)} %get-tuple-element.46), channel_id=1, source_target_pairs={{0,8},{1,9},{2,10},{3,11},{4,12},{5,13},{6,14},{7,15},{8,0},{9,1},... | collective-permute-start | bytes 208904 | tf_op jit(solution)/shard_map/ppermute | solution.py:302
  30.2 2.3 %collective-permute-start.6 = (bf16[136,256]{1,0:T(8,128)(2,1)S(1)}, bf16[136,256]{1,0:T(8,128)(2,1)S(1)}, u32[]{:S(2)}, u32[]{:S(2)}) collective-permute-start(bf16[136,256]{1,0:T(8,128)(2,1)S(1)} %get-tuple-element.47), channel_id=1, source_target_pairs={{0,16},{1,17},{2,18},{3,19},{4,20},{5,21},{6,22},{7,23},{8,24},{9,... | collective-permute-start | bytes 208904 | tf_op jit(solution)/shard_map/ppermute | solution.py:302
  32.5 0.1 collective-permute-start.7
  32.6 2.4 %collective-permute-done.6.p2 = bf16[136,256]{1,0:T(8,128)(2,1)S(1)} collective-permute-done((bf16[136,256]{1,0:T(8,128)(2,1)S(1)}, bf16[136,256]{1,0:T(8,128)(2,1)S(1)}, u32[]{:S(2)}, u32[]{:S(2)}) %collective-permute-start.6) | collective-permute-done | bytes 69664 | tf_op jit(solution)/shard_map/ppermute | solution.py:302
  35.0 2.8 %collective-permute-done.7.p3 = bf16[136,256]{1,0:T(8,128)(2,1)S(1)} collective-permute-done((bf16[136,256]{1,0:T(8,128)(2,1)S(1)}, bf16[136,256]{1,0:T(8,128)(2,1)S(1)}, u32[]{:S(2)}, u32[]{:S(2)}) %collective-permute-start.7) | collective-permute-done | bytes 69664 | tf_op jit(solution)/shard_map/ppermute | solution.py:302
  37.9 0.6 shard_map.97
  38.5 1.1 %collective-permute-start.10 = (bf16[128,256]{1,0:T(8,128)(2,1)S(1)}, bf16[128,256]{1,0:T(8,128)(2,1)S(1)}, u32[]{:S(2)}, u32[]{:S(2)}) collective-permute-start(bf16[128,256]{1,0:T(8,128)(2,1)S(1)} %get-tuple-element.52), channel_id=1, source_target_pairs={{0,24},{1,25},{2,26},{3,27},{4,28},{5,29},{6,30},{7,31},{8,16},{9,... | collective-permute-start | bytes 196616 | tf_op jit(solution)/shard_map/ppermute | solution.py:302
  39.6 2.5 %collective-permute-start.9 = (bf16[128,256]{1,0:T(8,128)(2,1)S(1)}, bf16[128,256]{1,0:T(8,128)(2,1)S(1)}, u32[]{:S(2)}, u32[]{:S(2)}) collective-permute-start(bf16[128,256]{1,0:T(8,128)(2,1)S(1)} %get-tuple-element.51), channel_id=1, source_target_pairs={{0,16},{1,17},{2,18},{3,19},{4,20},{5,21},{6,22},{7,23},{8,24},{9,... | collective-permute-start | bytes 196616 | tf_op jit(solution)/shard_map/ppermute | solution.py:302
  42.1 3.3 %shard_map.98.refs_0_ = f32[8,256,1024]{2,1,0:T(8,128)S(1)} custom-call(s32[3]{0:T(128)S(1)} %pad_add_fusion.ids.refs_0_, bf16[256,8192]{1,0:T(8,128)(2,1)} %gate_ref.3, bf16[128,256]{1,0:T(8,128)(2,1)S(1)} %get-tuple-element.49.refs_0_.e0), custom_call_target="tpu_custom_call" | custom-call | flops 1000000000 | bytes 4194304 | tf_op jit(solution)/shard_map/pallas_call | solution.py:403
  45.4 0.0 copy-start.3
  45.5 1.1 %shard_map.99 = (bf16[128,1024]{1,0:T(8,128)(2,1)S(1)}, bf16[128,1024]{1,0:T(8,128)(2,1)S(1)}, bf16[128,1024]{1,0:T(8,128)(2,1)S(1)}, bf16[128,1024]{1,0:T(8,128)(2,1)S(1)}) custom-call(s32[3]{0:T(128)S(1)} %pad_add_fusion.ids.refs_0_, bf16[128,256]{1,0:T(8,128)(2,1)S(1)} %get-tuple-element.49.refs_0_.e0, bf16[128,256]{1,0:T(8,128)(2,1)S(1)} %collective-permute-done.8.e1, ...), custom_call_target="tpu_custom_call" | custom-call | flops 2424832 | bytes 2424832 | tf_op jit(solution)/shard_map/pallas_call | solution.py:290
  46.6 2.2 %collective-permute-start.18 = (bf16[128,1024]{1,0:T(8,128)(2,1)S(1)}, bf16[128,1024]{1,0:T(8,128)(2,1)S(1)}, u32[]{:S(2)}, u32[]{:S(2)}) collective-permute-start(bf16[128,1024]{1,0:T(8,128)(2,1)S(1)} %get-tuple-element.60), channel_id=1, source_target_pairs={{0,6},{1,7},{2,4},{3,5},{4,2},{5,3},{6,0},{7,1},{8,14},{9,15},{10,... | collective-permute-start | bytes 786440 | tf_op jit(solution)/shard_map/ppermute | solution.py:302
  48.8 0.2 collective-permute-start.17
  49.1 0.2 collective-permute-start.15
  49.3 5.0 %collective-permute-start.21 = (bf16[128,1024]{1,0:T(8,128)(2,1)S(1)}, bf16[128,1024]{1,0:T(8,128)(2,1)S(1)}, u32[]{:S(2)}, u32[]{:S(2)}) collective-permute-start(bf16[128,1024]{1,0:T(8,128)(2,1)S(1)} %get-tuple-element.55.refs_1_.refs_4_.refs_8_), channel_id=1, source_target_pairs={{0,1},{1,0},{2,3},{3,2},{4,5},{5,4},{6,7},{7,6},{8,9},{9,8},{10,11... | collective-permute-start | bytes 786440 | tf_op jit(solution)/shard_map/ppermute | solution.py:302
  54.3 0.0 collective-permute-start.12
  54.3 1.2 %collective-permute-done.12 = f32[32]{0:T(128)S(1)} collective-permute-done((f32[32]{0:T(128)S(1)}, f32[32]{0:T(128)S(1)}, u32[]{:S(2)}, u32[]{:S(2)}) %collective-permute-start.12) | collective-permute-done | bytes 160 | tf_op jit(solution)/shard_map/ppermute | solution.py:302
  55.5 1.2 %collective-permute-start.13 = (f32[32]{0:T(128)S(1)}, f32[32]{0:T(128)S(1)}, u32[]{:S(2)}, u32[]{:S(2)}) collective-permute-start(f32[32]{0:T(128)S(1)} %copy-done.3), channel_id=1, source_target_pairs={{0,2},{1,3},{2,0},{3,1},{4,6},{5,7},{6,4},{7,5},{8,10},{9,11},{10,... | collective-permute-start | bytes 392 | tf_op jit(solution)/shard_map/ppermute | solution.py:302
  56.7 2.1 %collective-permute-done.13 = f32[32]{0:T(128)S(1)} collective-permute-done((f32[32]{0:T(128)S(1)}, f32[32]{0:T(128)S(1)}, u32[]{:S(2)}, u32[]{:S(2)}) %collective-permute-start.13) | collective-permute-done | bytes 160 | tf_op jit(solution)/shard_map/ppermute | solution.py:302
  58.8 4.3 %collective-permute-start.14 = (f32[32]{0:T(128)S(1)}, f32[32]{0:T(128)S(1)}, u32[]{:S(2)}, u32[]{:S(2)}) collective-permute-start(f32[32]{0:T(128)S(1)} %copy-done.3), channel_id=1, source_target_pairs={{0,3},{1,2},{2,1},{3,0},{4,7},{5,6},{6,5},{7,4},{8,11},{9,10},{10,... | collective-permute-start | bytes 392 | tf_op jit(solution)/shard_map/ppermute | solution.py:302
  63.1 1.3 %collective-permute-done.14 = f32[32]{0:T(128)S(1)} collective-permute-done((f32[32]{0:T(128)S(1)}, f32[32]{0:T(128)S(1)}, u32[]{:S(2)}, u32[]{:S(2)}) %collective-permute-start.14) | collective-permute-done | bytes 160 | tf_op jit(solution)/shard_map/ppermute | solution.py:302
  64.4 0.8 shard_map.101.refs_7_
  65.2 0.0 copy-start.2
  65.2 0.7 collective-permute-start.19
  65.9 0.1 collective-permute-start.20
  66.0 3.3 %shard_map.100.refs_4_ = f32[8,256,1024]{2,1,0:T(8,128)S(1)} custom-call(s32[3]{0:T(128)S(1)} %pad_add_fusion.ids.refs_0_, bf16[256,8192]{1,0:T(8,128)(2,1)} %gate_ref.3, f32[8,256,1024]{2,1,0:T(8,128)S(1)} %shard_map.98.refs_0_, bf16[128,1024]{1,0:T(8,128)(2,1)S(1)} %get-tuple-element.55.refs_1_.refs_4_.refs_8_), custom_call_target="tpu_custom_call", output_to_operand_aliasing={{}: (2, {})} | custom-call | flops 1000000000 | bytes 4194304 | tf_op jit(solution)/shard_map/pallas_call | solution.py:403
  69.3 0.5 collective-permute-start.16
  69.8 2.8 %shard_map.102.refs_10_ = bf16[256,8192]{1,0:T(8,128)(2,1)} custom-call(s32[3]{0:T(128)S(1)} %pad_add_fusion.ids.refs_0_, bf16[256,8192]{1,0:T(8,128)(2,1)S(1)} %copy-done, f32[8,256,1024]{2,1,0:T(8,128)S(1)} %get-tuple-element.37.refs_0_.refs_2_, f32[8,256,1024]{2,1,0:T(8,128)S(1)} %get-tuple-element.38.refs_3_, f32[8,256,1024]{2,1,0:T(8,128)S(1)} %shard_map.100.refs_4_, ...), custom_call_target="tpu_custom_call" | custom-call | flops 1000000000 | bytes 4194304 | tf_op jit(solution)/shard_map/pallas_call | solution.py:580
  72.6 2.0 %shard_map.103.refs_16_ = bf16[256,8192]{1,0:T(8,128)(2,1)} custom-call(s32[3]{0:T(128)S(1)} %pad_add_fusion.ids.refs_0_, bf16[256,8192]{1,0:T(8,128)(2,1)S(1)} %copy-done, f32[8,256,1024]{2,1,0:T(8,128)S(1)} %get-tuple-element.37.refs_0_.refs_2_, f32[8,256,1024]{2,1,0:T(8,128)S(1)} %get-tuple-element.38.refs_3_, ...), custom_call_target="tpu_custom_call", output_to_operand_aliasing={{}: (10, {})} | custom-call | flops 1000000000 | bytes 4194304 | tf_op jit(solution)/shard_map/pallas_call | solution.py:580
  74.6 4.3 %shard_map.104.refs_10_ = bf16[256,8192]{1,0:T(8,128)(2,1)} custom-call(s32[3]{0:T(128)S(1)} %pad_add_fusion.ids.refs_0_, bf16[256,8192]{1,0:T(8,128)(2,1)S(1)} %copy-done, f32[8,256,1024]{2,1,0:T(8,128)S(1)} %get-tuple-element.37.refs_0_.refs_2_, f32[8,256,1024]{2,1,0:T(8,128)S(1)} %get-tuple-element.38.refs_3_, ...), custom_call_target="tpu_custom_call", output_to_operand_aliasing={{}: (16, {})} | custom-call | flops 1000000000 | bytes 4194304 | tf_op jit(solution)/shard_map/pallas_call | solution.py:580
  79.0 2.0 %shard_map.105 = bf16[256,8192]{1,0:T(8,128)(2,1)} custom-call(s32[3]{0:T(128)S(1)} %pad_add_fusion.ids.refs_0_, bf16[256,8192]{1,0:T(8,128)(2,1)S(1)} %copy-done, f32[8,256,1024]{2,1,0:T(8,128)S(1)} %get-tuple-element.37.refs_0_.refs_2_, f32[8,256,1024]{2,1,0:T(8,128)S(1)} %get-tuple-element.38.refs_3_, ...), custom_call_target="tpu_custom_call", output_to_operand_aliasing={{}: (10, {})} | custom-call | flops 1000000000 | bytes 4194304 | tf_op jit(solution)/shard_map/pallas_call | solution.py:580
  (22 shorter events, 0.1 us)
Async XLA Ops:
  0.0 4.3 %copy-start.1 = (bf16[368,1024]{1,0:T(8,128)(2,1)S(1)}, bf16[368,1024]{1,0:T(8,128)(2,1)}, u32[]{:S(2)}) copy-start(bf16[368,1024]{1,0:T(8,128)(2,1)} %constant.17.clone.table_ref.refs_4_) | copy-start | bytes 2260996
  0.0 4.3 %copy-start = (bf16[256,8192]{1,0:T(8,128)(2,1)S(1)}, bf16[256,8192]{1,0:T(8,128)(2,1)}, u32[]{:S(2)}) copy-start(bf16[256,8192]{1,0:T(8,128)(2,1)} %refs_1_.7) | copy-start | bytes 12582916
  4.3 2.5 %collective-permute-start.1 = (bf16[2,136,1024]{2,1,0:T(8,128)(2,1)S(1)}, bf16[2,136,1024]{2,1,0:T(8,128)(2,1)S(1)}, u32[]{:S(2)}, u32[]{:S(2)}) collective-permute-start(bf16[2,136,1024]{2,1,0:T(8,128)(2,1)S(1)} %get-tuple-element.39), channel_id=1, source_target_pairs={{0,1},{1,0},{2,3},{3,2},{4,5},{5,4},{6,7},{7,6},{8,9},{9,8},{10,11... | collective-permute-start | bytes 1671176 | tf_op jit(solution)/shard_map/ppermute | solution.py:302
  6.2 2.6 %collective-permute-start = (bf16[2,136,1024]{2,1,0:T(8,128)(2,1)S(1)}, bf16[2,136,1024]{2,1,0:T(8,128)(2,1)S(1)}, u32[]{:S(2)}, u32[]{:S(2)}) collective-permute-start(bf16[2,136,1024]{2,1,0:T(8,128)(2,1)S(1)} %shard_map.93), channel_id=1, source_target_pairs={{0,1},{1,0},{2,3},{3,2},{4,5},{5,4},{6,7},{7,6},{8,9},{9,8},{10,11... | collective-permute-start | bytes 1671176 | tf_op jit(solution)/shard_map/ppermute | solution.py:302
  8.8 5.6 %copy-start.4 = (bf16[256,8,128]{2,1,0:T(8,128)(2,1)S(1)}, bf16[256,8,128]{2,1,0:T(8,128)(2,1)}, u32[]{:S(2)}) copy-start(bf16[256,8,128]{2,1,0:T(8,128)(2,1)} %c_ref.1) | copy-start | bytes 1572868
  10.9 12.6 %collective-permute-start.2 = (bf16[136,1024]{1,0:T(8,128)(2,1)S(1)}, bf16[136,1024]{1,0:T(8,128)(2,1)S(1)}, u32[]{:S(2)}, u32[]{:S(2)}) collective-permute-start(bf16[136,1024]{1,0:T(8,128)(2,1)S(1)} %get-tuple-element.42), channel_id=1, source_target_pairs={{0,2},{1,3},{2,0},{3,1},{4,6},{5,7},{6,4},{7,5},{8,10},{9,11},{10,... | collective-permute-start | bytes 835592 | tf_op jit(solution)/shard_map/ppermute | solution.py:302
  13.2 10.3 %collective-permute-start.3 = (bf16[136,1024]{1,0:T(8,128)(2,1)S(1)}, bf16[136,1024]{1,0:T(8,128)(2,1)S(1)}, u32[]{:S(2)}, u32[]{:S(2)}) collective-permute-start(bf16[136,1024]{1,0:T(8,128)(2,1)S(1)} %get-tuple-element.43), channel_id=1, source_target_pairs={{0,4},{1,5},{2,6},{3,7},{4,0},{5,1},{6,2},{7,3},{8,12},{9,13},{10,... | collective-permute-start | bytes 835592 | tf_op jit(solution)/shard_map/ppermute | solution.py:302
  14.4 12.3 %collective-permute-start.4 = (bf16[136,1024]{1,0:T(8,128)(2,1)S(1)}, bf16[136,1024]{1,0:T(8,128)(2,1)S(1)}, u32[]{:S(2)}, u32[]{:S(2)}) collective-permute-start(bf16[136,1024]{1,0:T(8,128)(2,1)S(1)} %get-tuple-element.44), channel_id=1, source_target_pairs={{0,6},{1,7},{2,4},{3,5},{4,2},{5,3},{6,0},{7,1},{8,14},{9,15},{10,... | collective-permute-start | bytes 835592 | tf_op jit(solution)/shard_map/ppermute | solution.py:302
  27.7 17.7 %collective-permute-start.11 = (bf16[4,136,1024]{2,1,0:T(8,128)(2,1)S(1)}, bf16[4,136,1024]{2,1,0:T(8,128)(2,1)S(1)}, u32[]{:S(2)}, u32[]{:S(2)}) collective-permute-start(bf16[4,136,1024]{2,1,0:T(8,128)(2,1)S(1)} %get-tuple-element.54), channel_id=1, source_target_pairs={{0,1},{2,3},{4,5},{6,7},{8,9},{10,11},{12,13},{14,15},{16,17},{18,... | collective-permute-start | bytes 3342344 | tf_op jit(solution)/shard_map/ppermute | solution.py:530
  29.0 3.6 %collective-permute-start.5 = (bf16[136,256]{1,0:T(8,128)(2,1)S(1)}, bf16[136,256]{1,0:T(8,128)(2,1)S(1)}, u32[]{:S(2)}, u32[]{:S(2)}) collective-permute-start(bf16[136,256]{1,0:T(8,128)(2,1)S(1)} %get-tuple-element.46), channel_id=1, source_target_pairs={{0,8},{1,9},{2,10},{3,11},{4,12},{5,13},{6,14},{7,15},{8,0},{9,1},... | collective-permute-start | bytes 208904 | tf_op jit(solution)/shard_map/ppermute | solution.py:302
  30.2 4.8 %collective-permute-start.6 = (bf16[136,256]{1,0:T(8,128)(2,1)S(1)}, bf16[136,256]{1,0:T(8,128)(2,1)S(1)}, u32[]{:S(2)}, u32[]{:S(2)}) collective-permute-start(bf16[136,256]{1,0:T(8,128)(2,1)S(1)} %get-tuple-element.47), channel_id=1, source_target_pairs={{0,16},{1,17},{2,18},{3,19},{4,20},{5,21},{6,22},{7,23},{8,24},{9,... | collective-permute-start | bytes 208904 | tf_op jit(solution)/shard_map/ppermute | solution.py:302
  32.5 5.3 %collective-permute-start.7 = (bf16[136,256]{1,0:T(8,128)(2,1)S(1)}, bf16[136,256]{1,0:T(8,128)(2,1)S(1)}, u32[]{:S(2)}, u32[]{:S(2)}) collective-permute-start(bf16[136,256]{1,0:T(8,128)(2,1)S(1)} %get-tuple-element.48), channel_id=1, source_target_pairs={{0,24},{1,25},{2,26},{3,27},{4,28},{5,29},{6,30},{7,31},{8,16},{9,... | collective-permute-start | bytes 208904 | tf_op jit(solution)/shard_map/ppermute | solution.py:302
  38.5 6.9 %collective-permute-start.10 = (bf16[128,256]{1,0:T(8,128)(2,1)S(1)}, bf16[128,256]{1,0:T(8,128)(2,1)S(1)}, u32[]{:S(2)}, u32[]{:S(2)}) collective-permute-start(bf16[128,256]{1,0:T(8,128)(2,1)S(1)} %get-tuple-element.52), channel_id=1, source_target_pairs={{0,24},{1,25},{2,26},{3,27},{4,28},{5,29},{6,30},{7,31},{8,16},{9,... | collective-permute-start | bytes 196616 | tf_op jit(solution)/shard_map/ppermute | solution.py:302
  39.6 5.8 %collective-permute-start.8 = (bf16[128,256]{1,0:T(8,128)(2,1)S(1)}, bf16[128,256]{1,0:T(8,128)(2,1)S(1)}, u32[]{:S(2)}, u32[]{:S(2)}) collective-permute-start(bf16[128,256]{1,0:T(8,128)(2,1)S(1)} %get-tuple-element.50), channel_id=1, source_target_pairs={{0,8},{1,9},{2,10},{3,11},{4,12},{5,13},{6,14},{7,15},{8,0},{9,1},... | collective-permute-start | bytes 196616 | tf_op jit(solution)/shard_map/ppermute | solution.py:302
  39.6 5.8 %collective-permute-start.9 = (bf16[128,256]{1,0:T(8,128)(2,1)S(1)}, bf16[128,256]{1,0:T(8,128)(2,1)S(1)}, u32[]{:S(2)}, u32[]{:S(2)}) collective-permute-start(bf16[128,256]{1,0:T(8,128)(2,1)S(1)} %get-tuple-element.51), channel_id=1, source_target_pairs={{0,16},{1,17},{2,18},{3,19},{4,20},{5,21},{6,22},{7,23},{8,24},{9,... | collective-permute-start | bytes 196616 | tf_op jit(solution)/shard_map/ppermute | solution.py:302
  45.4 8.9 %copy-start.3 = (f32[32]{0:T(128)S(1)}, f32[32]{0:T(128)}, u32[]{:S(2)}) copy-start(f32[32]{0:T(128)} %param.15) | copy-start | bytes 388
  46.6 18.6 %collective-permute-start.18 = (bf16[128,1024]{1,0:T(8,128)(2,1)S(1)}, bf16[128,1024]{1,0:T(8,128)(2,1)S(1)}, u32[]{:S(2)}, u32[]{:S(2)}) collective-permute-start(bf16[128,1024]{1,0:T(8,128)(2,1)S(1)} %get-tuple-element.60), channel_id=1, source_target_pairs={{0,6},{1,7},{2,4},{3,5},{4,2},{5,3},{6,0},{7,1},{8,14},{9,15},{10,... | collective-permute-start | bytes 786440 | tf_op jit(solution)/shard_map/ppermute | solution.py:302
  48.8 17.1 %collective-permute-start.17 = (bf16[128,1024]{1,0:T(8,128)(2,1)S(1)}, bf16[128,1024]{1,0:T(8,128)(2,1)S(1)}, u32[]{:S(2)}, u32[]{:S(2)}) collective-permute-start(bf16[128,1024]{1,0:T(8,128)(2,1)S(1)} %get-tuple-element.59), channel_id=1, source_target_pairs={{0,4},{1,5},{2,6},{3,7},{4,0},{5,1},{6,2},{7,3},{8,12},{9,13},{10,... | collective-permute-start | bytes 786440 | tf_op jit(solution)/shard_map/ppermute | solution.py:302
  49.1 20.2 %collective-permute-start.15 = (bf16[128,1024]{1,0:T(8,128)(2,1)S(1)}, bf16[128,1024]{1,0:T(8,128)(2,1)S(1)}, u32[]{:S(2)}, u32[]{:S(2)}) collective-permute-start(bf16[128,1024]{1,0:T(8,128)(2,1)S(1)} %get-tuple-element.58), channel_id=1, source_target_pairs={{0,2},{1,3},{2,0},{3,1},{4,6},{5,7},{6,4},{7,5},{8,10},{9,11},{10,... | collective-permute-start | bytes 786440 | tf_op jit(solution)/shard_map/ppermute | solution.py:302
  49.3 20.5 %collective-permute-start.21 = (bf16[128,1024]{1,0:T(8,128)(2,1)S(1)}, bf16[128,1024]{1,0:T(8,128)(2,1)S(1)}, u32[]{:S(2)}, u32[]{:S(2)}) collective-permute-start(bf16[128,1024]{1,0:T(8,128)(2,1)S(1)} %get-tuple-element.55.refs_1_.refs_4_.refs_8_), channel_id=1, source_target_pairs={{0,1},{1,0},{2,3},{3,2},{4,5},{5,4},{6,7},{7,6},{8,9},{9,8},{10,11... | collective-permute-start | bytes 786440 | tf_op jit(solution)/shard_map/ppermute | solution.py:302
  54.3 1.2 %collective-permute-start.12 = (f32[32]{0:T(128)S(1)}, f32[32]{0:T(128)S(1)}, u32[]{:S(2)}, u32[]{:S(2)}) collective-permute-start(f32[32]{0:T(128)S(1)} %copy-done.3), channel_id=1, source_target_pairs={{0,1},{1,0},{2,3},{3,2},{4,5},{5,4},{6,7},{7,6},{8,9},{9,8},{10,11... | collective-permute-start | bytes 392 | tf_op jit(solution)/shard_map/ppermute | solution.py:302
  55.5 3.3 %collective-permute-start.13 = (f32[32]{0:T(128)S(1)}, f32[32]{0:T(128)S(1)}, u32[]{:S(2)}, u32[]{:S(2)}) collective-permute-start(f32[32]{0:T(128)S(1)} %copy-done.3), channel_id=1, source_target_pairs={{0,2},{1,3},{2,0},{3,1},{4,6},{5,7},{6,4},{7,5},{8,10},{9,11},{10,... | collective-permute-start | bytes 392 | tf_op jit(solution)/shard_map/ppermute | solution.py:302
  58.8 5.6 %collective-permute-start.14 = (f32[32]{0:T(128)S(1)}, f32[32]{0:T(128)S(1)}, u32[]{:S(2)}, u32[]{:S(2)}) collective-permute-start(f32[32]{0:T(128)S(1)} %copy-done.3), channel_id=1, source_target_pairs={{0,3},{1,2},{2,1},{3,0},{4,7},{5,6},{6,5},{7,4},{8,11},{9,10},{10,... | collective-permute-start | bytes 392 | tf_op jit(solution)/shard_map/ppermute | solution.py:302
  65.2 4.6 %copy-start.2 = (f32[8192]{0:T(1024)S(1)}, f32[8192]{0:T(1024)}, u32[]{:S(2)}) copy-start(f32[8192]{0:T(1024)} %param.16) | copy-start | bytes 98308
  65.2 9.4 %collective-permute-start.19 = (bf16[128,1024]{1,0:T(8,128)(2,1)S(1)}, bf16[128,1024]{1,0:T(8,128)(2,1)S(1)}, u32[]{:S(2)}, u32[]{:S(2)}) collective-permute-start(bf16[128,1024]{1,0:T(8,128)(2,1)S(1)} %collective-permute-done.18.refs_8_), channel_id=1, source_target_pairs={{0,1},{1,0},{2,3},{3,2},{4,5},{5,4},{6,7},{7,6},{8,9},{9,8},{10,11... | collective-permute-start | bytes 786440 | tf_op jit(solution)/shard_map/ppermute | solution.py:302
  65.9 8.7 %collective-permute-start.20 = (bf16[128,1024]{1,0:T(8,128)(2,1)S(1)}, bf16[128,1024]{1,0:T(8,128)(2,1)S(1)}, u32[]{:S(2)}, u32[]{:S(2)}) collective-permute-start(bf16[128,1024]{1,0:T(8,128)(2,1)S(1)} %collective-permute-done.17.refs_8_), channel_id=1, source_target_pairs={{0,1},{1,0},{2,3},{3,2},{4,5},{5,4},{6,7},{7,6},{8,9},{9,8},{10,11... | collective-permute-start | bytes 786440 | tf_op jit(solution)/shard_map/ppermute | solution.py:302
  69.3 9.7 %collective-permute-start.16 = (bf16[128,1024]{1,0:T(8,128)(2,1)S(1)}, bf16[128,1024]{1,0:T(8,128)(2,1)S(1)}, u32[]{:S(2)}, u32[]{:S(2)}) collective-permute-start(bf16[128,1024]{1,0:T(8,128)(2,1)S(1)} %collective-permute-done.15.refs_9_), channel_id=1, source_target_pairs={{0,1},{1,0},{2,3},{3,2},{4,5},{5,4},{6,7},{7,6},{8,9},{9,8},{10,11... | collective-permute-start | bytes 786440 | tf_op jit(solution)/shard_map/ppermute | solution.py:302
where the time goes:
time: 81.2 us; the launch traced here: 81 us
  Pallas kernels  40.4 us (50%)
  starting transfers between devices  27.3 us (34%)
  waiting for transfers between devices  12.9 us (16%)
    ppermute x21, starting transfers between devices, exchange(): return lax.ppermute(value, AXES, [(i, i ^ mask) for i in range(count)])  26 us
    pallas_call x7, Pallas kernels, call(): pl.pallas_call(kernel, grid_spec=pltpu.PrefetchScalarGridSpec(num_scalar_...  25.7 us
    ppermute x21, waiting for transfers between devices, exchange(): return lax.ppermute(value, AXES, [(i, i ^ mask) for i in range(count)])  12.9 us
    pallas_call x4, Pallas kernels, finish(): pl.pallas_call(kernel, out_shape=out(rows, inner), in_specs=[SM] + [VM] *...  11.2 us
    pallas_call x4, Pallas kernels, small_call(): pl.pallas_call(kernel, out_shape=outs, in_specs=[SM] + [VM] * len(args) +...  3.55 us
  transfers between devices with their start and end apart: 22, of which 6 were waited for; matrix products, arithmetic and copies ran while one was open for 0% of the time, Pallas kernels for 37%

commit v1 on v0

--- a/solution.py
+++ b/solution.py
@@ -97,8 +97,16 @@
     sc_ref[:, heads:] = low
 
 
-def scaled_features(x_ref, sx_ref, spread):
-    return (x_ref[...].astype(F32) * dot(sx_ref[...], spread)).astype(BF16)
+def scaled_features(x, sx_ref, spread):
+    return (x.astype(F32) * dot(sx_ref[...], spread)).astype(BF16)
+
+
+def rows_of(ref, group, groups):
+    return ref[pl.ds(group, ref.shape[0] // groups, stride=groups), :].astype(BF16)
+
+
+def columns_of(group, width):
+    return pl.ds(pl.multiple_of(group * width, width), width)
 
 
 def update_of(xa, b_group, scalars):
@@ -110,11 +118,11 @@
     return total
 
 
-def own_update(group, x_ref, bg_ref, sx_ref, sc_ref, table_ref):
-    groups = bg_ref.shape[0]
+def own_update(group, groups, x, b_ref, sx_ref, sc_ref, table_ref):
     spread = spread_of(table_ref, group, sx_ref.shape[1] // 2, groups)
     scalars = dot(sc_ref[...], spread)
-    return update_of(scaled_features(x_ref, sx_ref, spread), bg_ref[group], scalars), scalars[0:1]
+    xa = scaled_features(x, sx_ref, spread)
+    return update_of(xa, rows_of(b_ref, group, groups), scalars), scalars[0:1]
 
 
 def away_group(ids, slot, groups):
@@ -130,43 +138,50 @@
     put_decay(ref, decay)
 
 
-def first_kernel(
-    ids, x_ref, b_ref, step_ref, decay_ref, table_ref, u_ref, bg_ref, sx_ref, sr_ref, sc_ref, b32
-):
-    i = pl.program_id(0)
+def first_kernel(slots, ids, x_far, b_far, step_far, decay_far, table_far, *refs):
+    u_ref, b32, sx_ref, sr_ref, sc_ref, x_ref, b_ref, step_ref, decay_ref, table_ref, sems = refs
     rows, groups, state = b_ref.shape
-
-    @pl.when(i == 0)
-    def _():
-        write_scales(decay_ref, step_ref, sx_ref, sr_ref, sc_ref)
-        b32[...] = b_ref[...].astype(F32).reshape(rows * groups, state)
-        for g in range(groups):
-            bg_ref[g] = b32[pl.ds(g, rows, stride=groups), :].astype(BF16)
-
-    group = away_group(ids, 3 - i, groups)
-    put_update(u_ref.at[0], *own_update(group, x_ref, bg_ref, sx_ref, sc_ref, table_ref))
-
-
-def second_kernel(ids, x_ref, bg_ref, sx_ref, sc_ref, table_ref, u_ref):
-    group = away_group(ids, 1 - pl.program_id(0), bg_ref.shape[0])
-    put_update(u_ref.at[0], *own_update(group, x_ref, bg_ref, sx_ref, sc_ref, table_ref))
-
-
-def home_kernel(slot, ids, x_ref, bg_ref, sx_ref, sc_ref, table_ref, far_ref, u_ref, p0, p1):
-    i = pl.program_id(0)
-    group = home_group(ids, slot - i, bg_ref.shape[0])
-    update, decay = own_update(group, x_ref, bg_ref, sx_ref, sc_ref, table_ref)
-    put_update(u_ref.at[0], update, decay)
-    far, far_decay = far_ref[0, :-EXTRA, :].astype(F32), decay_of(far_ref.at[0])
+    width = x_ref.shape[2]
+    places = [away_group(ids, m, groups) for m in slots]
+    pairs = [(decay_far, decay_ref), (step_far, step_ref), (b_far, b_ref), (table_far, table_ref)]
+    pairs += [(x_far.at[:, columns_of(g, width)], x_ref.at[i]) for i, g in enumerate(places)]
+    copies = [pltpu.make_async_copy(a, b, sems.at[i]) for i, (a, b) in enumerate(pairs)]
+    for copy in copies:
+        copy.start()
+    copies[0].wait()
+    copies[1].wait()
+    write_scales(decay_ref, step_ref, sx_ref, sr_ref, sc_ref)
+    copies[2].wait()
+    b32[...] = b_ref[...].astype(F32).reshape(rows * groups, state)
+    copies[3].wait()
+    for i, group in enumerate(places):
+        copies[4 + i].wait()
+        put_update(
+            u_ref.at[i], *own_update(group, groups, x_ref[i], b32, sx_ref, sc_ref, table_ref)
+        )
+
+
+def second_kernel(slots, groups, ids, x_ref, b_ref, sx_ref, sc_ref, table_ref, u_ref):
+    for i, m in enumerate(slots):
+        group = away_group(ids, m, groups)
+        x = x_ref[:, columns_of(group, u_ref.shape[2])]
+        put_update(u_ref.at[i], *own_update(group, groups, x, b_ref, sx_ref, sc_ref, table_ref))
+
+
+def home_kernel(slots, groups, ids, x_ref, b_ref, sx_ref, sc_ref, table_ref, far_ref, u_ref, *outs):
     late = ids[CORE].astype(F32)
-    joined = update * (late + (1.0 - late) * far_decay) + far * ((1.0 - late) + late * decay)
-    both = decay * far_decay
-    pl.when(i == 0)(lambda: put_update(p0, joined, both))
-    pl.when(i == 1)(lambda: put_update(p1, joined, both))
+    for i, m in enumerate(slots):
+        group = home_group(ids, m, groups)
+        x = x_ref[:, columns_of(group, u_ref.shape[2])]
+        update, decay = own_update(group, groups, x, b_ref, sx_ref, sc_ref, table_ref)
+        put_update(u_ref.at[i], update, decay)
+        far, far_decay = far_ref[i, :-EXTRA, :].astype(F32), decay_of(far_ref.at[i])
+        joined = update * (late + (1.0 - late) * far_decay) + far * ((1.0 - late) + late * decay)
+        put_update(outs[i], joined, decay * far_decay)
 
 
 def skip_kernel(ids, *refs):
-    pieces, out_ref = refs[:-2], refs[-1]
+    pieces, out_ref = refs[:-1], refs[-1]
     groups, _, width = out_ref.shape
     share = pieces[0].shape[1]
     heads = share * len(pieces)
@@ -182,44 +197,46 @@
             out_ref[(place ^ m) * spread_groups + k] = dot(high, pick) + dot(low, pick)
 
 
-def gate_kernel(gate_ref, out_ref):
-    half = 0.5 * gate_ref[...].astype(F32)
-    out_ref[0] = half + half * jnp.tanh(half)
+def gate_kernel(ids, gate_ref, out_ref):
+    groups, _, width = out_ref.shape
+    for group in range(groups):
+        half = 0.5 * gate_ref[:, group * width : (group + 1) * width].astype(F32)
+        out_ref[group] = half + half * jnp.tanh(half)
 
 
 def local_kernel(
-    ids, x_ref, c_ref, bg_ref, sx_ref, sr_ref, sc_ref, table_ref, y_ref, r_ref, cg_ref, c32
+    ids, x_ref, c_ref, b_ref, sx_ref, sr_ref, sc_ref, table_ref, y_ref, r_ref, cg_ref, c32
 ):
-    i = pl.program_id(0)
-    group = i
     rows, groups, state = c_ref.shape
+    width = y_ref.shape[2]
     heads = sx_ref.shape[1] // 2
     subs = rows // SUB
-
-    @pl.when(i == 0)
-    def _():
-        c32[...] = c_ref[...].astype(F32).reshape(rows * groups, state)
-
-    c_group = c32[pl.ds(group, rows, stride=groups), :].astype(BF16)
-    cg_ref[0] = c_group
-    spread = spread_of(table_ref, group, heads, groups)
-    scalars = dot(sc_ref[...], spread)
-    xa = scaled_features(x_ref, sx_ref, spread)
-    row_scale = dot(sr_ref[...], spread)
+    c32[...] = c_ref[...].astype(F32).reshape(rows * groups, state)
     row = lax.broadcasted_iota(jnp.int32, (SUB, SUB), 0)
     column = lax.broadcasted_iota(jnp.int32, (SUB, SUB), 1)
-    b_group = bg_ref[group]
-    for b in range(subs):
-        part = slice(b * SUB, (b + 1) * SUB)
-        scores = jnp.where(row >= column, dot_nt(c_group[part], b_group[part]), 0.0)
-        inner = dot(scores.astype(BF16), xa[part])
-        for a in range(b):
-            other = slice(a * SUB, (a + 1) * SUB)
-            scores = dot_nt(c_group[part], b_group[other]).astype(BF16)
-            at = pair_row(b, a, subs)
-            inner = inner + dot(scores, xa[other]) * scalars[at : at + 1]
-        y_ref[0, part, :] = row_scale[part] * inner
-        r_ref[0, part, :] = row_scale[part] * scalars[1 + subs + b : 2 + subs + b]
+
+    def one(group, carry):
+        c_group = rows_of(c32, group, groups)
+        cg_ref[group] = c_group
+        spread = spread_of(table_ref, group, heads, groups)
+        scalars = dot(sc_ref[...], spread)
+        xa = scaled_features(x_ref[:, columns_of(group, width)], sx_ref, spread)
+        row_scale = dot(sr_ref[...], spread)
+        b_group = rows_of(b_ref, group, groups)
+        for b in range(subs):
+            part = slice(b * SUB, (b + 1) * SUB)
+            scores = jnp.where(row >= column, dot_nt(c_group[part], b_group[part]), 0.0)
+            inner = dot(scores.astype(BF16), xa[part])
+            for a in range(b):
+                other = slice(a * SUB, (a + 1) * SUB)
+                scores = dot_nt(c_group[part], b_group[other]).astype(BF16)
+                at = pair_row(b, a, subs)
+                inner = inner + dot(scores, xa[other]) * scalars[at : at + 1]
+            y_ref[group, part, :] = row_scale[part] * inner
+            r_ref[group, part, :] = row_scale[part] * scalars[1 + subs + b : 2 + subs + b]
+        return carry
+
+    lax.fori_loop(0, groups, one, 0)
 
 
 def hold(held, place, pieces):
@@ -256,7 +273,7 @@
 def side_up_kernel(ids, p0, p1, p2, p3, *refs):
     o0, o1, o2, o3, held, state = refs[-6:]
     hold(held, ids[SIDE], (p0, p1, p2, p3))
-    if len(refs) == 8:
+    if len(refs) == 7:
         state[0] = refs[0][:-EXTRA, :]
     else:
         state[0] = jnp.zeros(state.shape[1:], BF16)
@@ -285,17 +302,25 @@
         out[...] = state[ids[CHIP] ^ m]
 
 
-def small_call(kernel, ids, args, outs, scratch=(), after=()):
-    size = sum(a.size * 2 for a in args) + sum(2 * o.size for o in outs)
+def small_call(kernel, ids, args, outs, scratch=(), after=(), far=(), reuse=0, cost=0, grant=8):
+    size = sum(a.size * 2 for a in (*args, *far)) + sum(2 * o.size for o in outs)
+
+    def body(ids, *refs):
+        given = len(far) + len(args)
+        kernel(ids, *refs[:given], *refs[given + len(after) :])
+
     return pl.pallas_call(
-        kernel,
+        body,
         out_shape=outs,
-        in_specs=[SM] + [VM] * len(args) + [ANY] * len(after),
+        in_specs=[SM] + [ANY] * len(far) + [VM] * len(args) + [ANY] * len(after),
         out_specs=[VM] * len(outs),
         scratch_shapes=list(scratch),
-        compiler_params=pltpu.CompilerParams(vmem_limit_bytes=8 * MIB),
-        cost_estimate=pl.CostEstimate(flops=size, bytes_accessed=size, transcendentals=0),
-    )(ids, *args, *after)
+        input_output_aliases={1 + len(far) + len(args) + n: n for n in range(reuse)},
+        compiler_params=pltpu.CompilerParams(vmem_limit_bytes=grant * MIB),
+        cost_estimate=pl.CostEstimate(
+            flops=size + cost * 10**9, bytes_accessed=size, transcendentals=0
+        ),
+    )(ids, *far, *args, *after)
 
 
 def exchange(value, mask, count):
@@ -393,124 +418,66 @@
     def out(*shape, kind=BF16):
         return jax.ShapeDtypeStruct(shape, kind)
 
-    def whole(*shape):
-        return pl.BlockSpec(shape, lambda i, *_: (0,) * len(shape))
-
-    def block(place):
-        return pl.BlockSpec((rows, width), lambda i, ids: (0, place(ids, i)))
-
-    def call(kernel, steps, in_specs, out_specs, outs, args, scratch=(), aliases=None, cost=1, grant=8):
-        return pl.pallas_call(
-            kernel,
-            grid_spec=pltpu.PrefetchScalarGridSpec(
-                num_scalar_prefetch=1,
-                grid=(steps,),
-                in_specs=in_specs,
-                out_specs=out_specs,
-                scratch_shapes=list(scratch),
-            ),
-            out_shape=outs,
-            input_output_aliases=aliases or {},
-            compiler_params=pltpu.CompilerParams(vmem_limit_bytes=grant * MIB),
-            cost_estimate=pl.CostEstimate(
-                flops=cost * 10**9, bytes_accessed=cost * 4 * 2**20, transcendentals=0
-            ),
-        )(ids, *args)
-
-    slot_spec = pl.BlockSpec((1, tall, width), lambda i, *_: (i, 0, 0))
-    sx_spec, sc_spec = whole(rows, 2 * heads), whole(EXTRA, 2 * heads)
-    table_spec, bg_spec = whole(*table.shape), whole(groups, rows, state)
-    chunk = out(2, tall, width)
-
-    away32, bg, sx, sr, sc = call(
-        first_kernel,
-        2,
+    rows_kind, scale_kind = out(rows * groups, state, kind=F32), out(rows, 2 * heads)
+    piece = out(tall, width)
+    head_slots, rest_slots = (3,), (2, 1, 0)
+
+    def bound(kernel, *given):
+        return lambda *refs: kernel(*given, *refs)
+
+    away3, b_rows, sx, sr, sc = small_call(
+        bound(first_kernel, head_slots),
+        ids,
+        (),
+        [out(1, tall, width), rows_kind, scale_kind, scale_kind, out(EXTRA, 2 * heads)],
         [
-            block(lambda ids, i: away_group(ids, 3 - i, groups)),
-            whole(rows, groups, state),
-            whole(rows, heads),
-            whole(rows, heads),
-            table_spec,
+            pltpu.VMEM((1, rows, width), BF16),
+            pltpu.VMEM((rows, groups, state), BF16),
+            pltpu.VMEM((rows, heads), F32),
+            pltpu.VMEM((rows, heads), F32),
+            pltpu.VMEM(table.shape, BF16),
+            pltpu.SemaphoreType.DMA((5,)),
         ],
-        [slot_spec, bg_spec, sx_spec, sx_spec, sc_spec],
-        [chunk, out(groups, rows, state), *[out(rows, 2 * heads)] * 2, out(EXTRA, 2 * heads)],
-        far_memory(features, bmat, step_size, log_decay, table),
-        [pltpu.VMEM((rows * groups, state), F32)],
-    )
-    far32 = exchange(away32, 1, count)
-    (away10,) = call(
-        second_kernel,
-        2,
-        [
-            block(lambda ids, i: away_group(ids, 1 - i, groups)),
-            bg_spec,
-            sx_spec,
-            sc_spec,
-            table_spec,
-        ],
-        [slot_spec],
-        [chunk],
-        (features, bg, sx, sc, table),
-    )
-    far10 = exchange(away10, 1, count)
-
-    def home(slot, far, earlier):
-        def kernel(ids, *refs):
-            home_kernel(slot, ids, *refs[:6], *refs[6 + len(earlier) :])
-
-        half_spec = pl.BlockSpec((1, tall, width), lambda i, ids: (3 - slot + i, 0, 0))
-
-        return call(
-            kernel,
-            2,
-            [
-                block(lambda ids, i: home_group(ids, slot - i, groups)),
-                bg_spec,
-                sx_spec,
-                sc_spec,
-                table_spec,
-                slot_spec,
-            ]
-            + [ANY] * len(earlier),
-            [half_spec, whole(tall, width), whole(tall, width)],
-            [out(PLANE, tall, width), out(tall, width), out(tall, width)],
-            (features, bg, sx, sc, table, far, *earlier),
-            aliases={7: 0} if earlier else {},
+        far=far_memory(features, bmat, step_size, log_decay, table),
+        cost=1,
+        grant=10,
+    )
+    far3 = exchange(away3, 1, count)
+    (away210,) = small_call(
+        bound(second_kernel, rest_slots, groups),
+        ids,
+        (features, b_rows, sx, sc, table),
+        [out(3, tall, width)],
+        cost=1,
+    )
+    far210 = exchange(away210, 1, count)
+
+    def home(slots, far):
+        return small_call(
+            bound(home_kernel, slots, groups),
+            ids,
+            (features, b_rows, sx, sc, table, far),
+            [out(len(slots), tall, width)] + [piece] * len(slots),
+            cost=1,
         )
 
-    own, piece3, piece2 = home(3, far32, ())
+    own3, piece3 = home(head_slots, far3)
     moved3 = exchange(piece3, 6, count)
+    own210, piece2, piece1, piece0 = home(rest_slots, far210)
     moved2 = exchange(piece2, 4, count)
-    own, piece1, piece0 = home(1, far10, (own,))
-    pieces = [piece0, exchange(piece1, 2, count), moved2, moved3]
-
-    group_block = pl.BlockSpec((1, rows, width), lambda i, ids: (i, 0, 0))
-    y, r, cg = call(
+    moved1 = exchange(piece1, 2, count)
+    pieces = [piece0, moved1, moved2, moved3]
+
+    large = out(groups, rows, width, kind=F32)
+    y, r, cg = small_call(
         local_kernel,
-        groups,
-        [block(lambda ids, i: i), whole(rows, groups, state), bg_spec]
-        + [sx_spec, sx_spec, sc_spec, table_spec],
-        [group_block, group_block, pl.BlockSpec((1, rows, state), lambda i, ids: (i, 0, 0))],
-        [out(groups, rows, width, kind=F32)] * 2 + [out(groups, rows, state)],
-        (features, cmat, bg, sx, sr, sc, table),
+        ids,
+        (features, cmat, b_rows, sx, sr, sc, table),
+        [large, large, out(groups, rows, state)],
         [pltpu.VMEM((rows * groups, state), F32)],
         cost=4,
-        grant=14,
-    )
-
-    def gate(slot, earlier, after):
-        def place(ids, i):
-            return (ids[CORE] ^ (i & 1)) * (groups // 2) + (ids[CHIP] ^ (slot + i // 2))
-
-        return call(
-            lambda ids, gate_ref, *refs: gate_kernel(gate_ref, refs[-1]),
-            4,
-            [block(place)] + [ANY] * (len(earlier) + 1),
-            [pl.BlockSpec((1, rows, width), lambda i, ids: (place(ids, i), 0, 0))],
-            [out(groups, rows, width, kind=F32)],
-            (*far_memory(gate_input), *earlier, after),
-            aliases={2: 0} if earlier else {},
-        )
+        grant=10,
+    )
 
     quarters = small_call(
         plane_down_kernel,
@@ -526,8 +493,9 @@
     for m in range(1, heads // skip.shape[0]):
         skips.append(exchange(skip, m, count))
     skips = [v.reshape(1, v.shape[0]) for v in skips]
-    lacking, _ = lax.optimization_barrier((own, quarters[0]))
-    lacking = lax.ppermute(lacking, AXES, [(i, i + 1) for i in range(0, count, 2)])
+    early = [(i, i + 1) for i in range(0, count, 2)]
+    lack3, lack210, _ = lax.optimization_barrier((own3, own210, quarters[0]))
+    lack3, lack210 = (lax.ppermute(v, AXES, early) for v in (lack3, lack210))
     side_scratch = [
         pltpu.VMEM((PLANE, tall, width // PLANE), BF16),
         pltpu.VMEM((PLANE, state, width // PLANE), BF16),
@@ -546,7 +514,10 @@
         [out(state, width // PLANE)] * PLANE,
         side_scratch,
     )
-    gates = gate(0, (), entering[0])
+    (gates,) = small_call(gate_kernel, ids, (gate_input,), [large], after=[entering[0]], cost=2)
+    (skip_rows,) = small_call(
+        skip_kernel, ids, skips, [out(groups, EXTRA, width, kind=F32)], (), [entering[0]]
+    )
     entering = exchange_pieces(entering, 8, count)
     states = small_call(
         plane_up_kernel,
@@ -558,12 +529,9 @@
             pltpu.VMEM((PLANE, state, width), BF16),
             pltpu.VMEM((PLANE, state, width // PLANE), BF16),
         ],
-        [*gates, lacking],
+        [gates, skip_rows, lack3, lack210],
     )
     states = exchange_pieces(states, 2, count)
-    (skip_rows,) = small_call(
-        skip_kernel, ids, skips, [out(groups, EXTRA, width, kind=F32)], (), [states[0]]
-    )
     gain = norm_gain.reshape(1, inner)
     forwarded = []
     for s in states:
@@ -571,10 +539,10 @@
 
     def finish(entries, result):
         def kernel(*refs):
-            finish_kernel([(m, side, (3 - m) % (4 if side else 2)) for m, side in entries], *refs)
+            finish_kernel([(m, side, max(0, 2 - m)) for m, side in entries], *refs)
 
         given = [forwarded[m] if side else states[m] for m, side in entries]
-        updates = [lacking if side else far32 if m > 1 else far10 for m, side in entries]
+        updates = [((far210, far3), (lack210, lack3))[side][m == 3] for m, side in entries]
         earlier = [] if result is None else [result]
         args = (ids, features, y, r, gates, cg, gain, skip_rows, *given, *updates)
         return pl.pallas_call(
@@ -592,11 +560,11 @@
             cost_estimate=pl.CostEstimate(flops=10**9, bytes_accessed=4 * 2**20, transcendentals=0),
         )(*args, *earlier)
 
-    (gates,) = gate(2, gates, states[0])
-    result = finish([(0, 0), (0, 1)], None)
-    result = finish([(3, 0)], result)
-    result = finish([(2, 0), (1, 0), (3, 1), (2, 1)], result)
-    return finish([(1, 1)], result)
+    result = finish([(0, 0)], None)
+    result = finish([(0, 1), (1, 0)], result)
+    result = finish([(1, 1), (2, 0)], result)
+    result = finish([(2, 1), (3, 0)], result)
+    return finish([(3, 1)], result)
 
 
 def solution(mesh):

time: 81.2 us -> 78.2 us (0.963)
  starting transfers between devices: 27.3 us -> 33.7 us
  Pallas kernels: 40.4 us -> 35 us
  waiting for transfers between devices: 12.9 us -> 8.78 us
    pallas_call x11 -> x10, Pallas kernels: 29.2 us -> 22.6 us  [small_call(): pl.pallas_call(body, out_shape=outs, in_specs=[SM] + [ANY] * len(far) + [...]
    ppermute x21, starting transfers between devices: 26 us -> 31 us  [exchange(): return lax.ppermute(value, AXES, [(i, i ^ mask) for i in range(count)])]
    ppermute x21, waiting for transfers between devices: 12.9 us -> 8.77 us  [exchange(): return lax.ppermute(value, AXES, [(i, i ^ mask) for i in range(count)])]
    ppermute x1 -> x2, starting transfers between devices: 1.29 us -> 2.72 us  [shards(): lack3, lack210 = (lax.ppermute(v, AXES, early) for v in (lack3, lack210))]
    pallas_call x4 -> x5, Pallas kernels: 11.2 us -> 12.4 us  [finish(): pl.pallas_call(kernel, out_shape=out(rows, inner), in_specs=[SM] + [VM] *...]
  transfers between devices with their start and end apart: 22 -> 23, of which waited for: 6 -> 6; matrix products, arithmetic and copies ran while one was open for 0% -> 0% of each run, Pallas kernels for 37% -> 33%
where the time goes in v1:
time: 78.2 us; the launch traced here: 78 us
  Pallas kernels  35 us (45%)
  starting transfers between devices  33.7 us (43%)
  waiting for transfers between devices  8.78 us (11%)
    ppermute x21, starting transfers between devices, exchange(): return lax.ppermute(value, AXES, [(i, i ^ mask) for i in range(count)])  31 us
    pallas_call x10, Pallas kernels, small_call(): pl.pallas_call(body, out_shape=outs, in_specs=[SM] + [ANY] * len(far) + [...  22.6 us
    pallas_call x5, Pallas kernels, finish(): pl.pallas_call(kernel, out_shape=out(rows, inner), in_specs=[SM] + [VM] *...  12.4 us
    ppermute x21, waiting for transfers between devices, exchange(): return lax.ppermute(value, AXES, [(i, i ^ mask) for i in range(count)])  8.77 us
    ppermute x2, starting transfers between devices, shards(): lack3, lack210 = (lax.ppermute(v, AXES, early) for v in (lack3, lack210))  2.72 us
  transfers between devices with their start and end apart: 23, of which 6 were waited for; matrix products, arithmetic and copies ran while one was open for 0% of the time, Pallas kernels for 33%

profile of v1, /device:TPU:1, one launch (start us, length us, event | category | flops | bytes accessed | tf_op | source)
XLA Modules:
  0.0 78.0 jit_solution(18323999004442185141)
XLA Ops:
  0.0 0.1 pad_add_fusion.ids.refs_0_
  0.1 3.0 %shard_map.91 = (bf16[1,136,1024]{2,1,0:T(8,128)(2,1)S(1)}, f32[2048,128]{1,0:T(8,128)S(1)}, bf16[256,256]{1,0:T(8,128)(2,1)S(1)}, bf16[256,256]{1,0:T(8,128)(2,1)S(1)}, bf16[8,256]{1,0:T(8,128)(2,1)S(1)}) custom-call(s32[3]{0:T(128)S(1)} %pad_add_fusion.ids.refs_0_, bf16[256,8192]{1,0:T(8,128)(2,1)} %refs_1_.13, bf16[256,8,128]{2,1,0:T(8,128)(2,1)} %refs_1_.7, ...), custom_call_target="tpu_custom_call" | custom-call | flops 1006672384 | bytes 6672384 | tf_op jit(solution)/shard_map/pallas_call | solution.py:312
  3.1 2.0 %shard_map.93 = bf16[3,136,1024]{2,1,0:T(8,128)(2,1)S(1)} custom-call(s32[3]{0:T(128)S(1)} %pad_add_fusion.ids.refs_0_, bf16[256,8192]{1,0:T(8,128)(2,1)S(1)} %copy-done, f32[2048,128]{1,0:T(8,128)S(1)} %get-tuple-element.34.refs_2_.refs_1_, bf16[256,256]{1,0:T(8,128)(2,1)S(1)} %get-tuple-element.35.refs_3_.refs_2_, ...), custom_call_target="tpu_custom_call" | custom-call | flops 1006443008 | bytes 6443008 | tf_op jit(solution)/shard_map/pallas_call | solution.py:312
  5.2 0.1 collective-permute-start
  5.3 0.5 collective-permute-start.3
  5.8 2.2 %collective-permute-done.3.refs_5_.refs_11_ = bf16[1,136,1024]{2,1,0:T(8,128)(2,1)S(1)} collective-permute-done((bf16[1,136,1024]{2,1,0:T(8,128)(2,1)S(1)}, bf16[1,136,1024]{2,1,0:T(8,128)(2,1)S(1)}, u32[]{:S(2)}, u32[]{:S(2)}) %collective-permute-start.3) | collective-permute-done | bytes 278560 | tf_op jit(solution)/shard_map/ppermute | solution.py:327
  8.0 1.2 %shard_map.95 = (bf16[1,136,1024]{2,1,0:T(8,128)(2,1)S(1)}, bf16[136,1024]{1,0:T(8,128)(2,1)S(1)}) custom-call(s32[3]{0:T(128)S(1)} %pad_add_fusion.ids.refs_0_, bf16[256,8192]{1,0:T(8,128)(2,1)S(1)} %copy-done, f32[2048,128]{1,0:T(8,128)S(1)} %get-tuple-element.34.refs_2_.refs_1_, bf16[256,256]{1,0:T(8,128)(2,1)S(1)} %get-tuple-element.35.refs_3_.refs_2_, ...), custom_call_target="tpu_custom_call" | custom-call | flops 1006443008 | bytes 6443008 | tf_op jit(solution)/shard_map/pallas_call | solution.py:312
  9.2 0.0 copy-start.5
  9.2 3.4 %collective-permute-start.4 = (bf16[136,1024]{1,0:T(8,128)(2,1)S(1)}, bf16[136,1024]{1,0:T(8,128)(2,1)S(1)}, u32[]{:S(2)}, u32[]{:S(2)}) collective-permute-start(bf16[136,1024]{1,0:T(8,128)(2,1)S(1)} %get-tuple-element.44), channel_id=1, source_target_pairs={{0,6},{1,7},{2,4},{3,5},{4,2},{5,3},{6,0},{7,1},{8,14},{9,15},{10,... | collective-permute-start | bytes 835592 | tf_op jit(solution)/shard_map/ppermute | solution.py:327
  12.6 0.0 collective-permute-done.refs_5_.refs_9_.refs_11_
  12.6 2.2 %shard_map.94 = (bf16[3,136,1024]{2,1,0:T(8,128)(2,1)S(1)}, bf16[136,1024]{1,0:T(8,128)(2,1)S(1)}, bf16[136,1024]{1,0:T(8,128)(2,1)S(1)}, bf16[136,1024]{1,0:T(8,128)(2,1)S(1)}) custom-call(s32[3]{0:T(128)S(1)} %pad_add_fusion.ids.refs_0_, bf16[256,8192]{1,0:T(8,128)(2,1)S(1)} %copy-done, f32[2048,128]{1,0:T(8,128)S(1)} %get-tuple-element.34.refs_2_.refs_1_, ...), custom_call_target="tpu_custom_call" | custom-call | flops 1008114176 | bytes 8114176 | tf_op jit(solution)/shard_map/pallas_call | solution.py:312
  14.8 0.3 collective-permute-start.1
  15.1 0.1 collective-permute-start.2
  15.2 8.7 %shard_map.92 = (f32[8,256,1024]{2,1,0:T(8,128)S(1)}, f32[8,256,1024]{2,1,0:T(8,128)S(1)}, bf16[8,256,128]{2,1,0:T(8,128)(2,1)S(1)}) custom-call(s32[3]{0:T(128)S(1)} %pad_add_fusion.ids.refs_0_, bf16[256,8192]{1,0:T(8,128)(2,1)S(1)} %copy-done, bf16[256,8,128]{2,1,0:T(8,128)(2,1)S(1)} %copy-done.5, f32[2048,128]{1,0:T(8,128)S(1)} %get-tuple-element.34.refs_2_.refs_1_, ...), custom_call_target="tpu_custom_call" | custom-call | flops 4015175680 | bytes 15175680 | tf_op jit(solution)/shard_map/pallas_call | solution.py:312
  23.9 1.8 %collective-permute-done.1.refs_1_.refs_5_ = bf16[136,1024]{1,0:T(8,128)(2,1)S(1)} collective-permute-done((bf16[136,1024]{1,0:T(8,128)(2,1)S(1)}, bf16[136,1024]{1,0:T(8,128)(2,1)S(1)}, u32[]{:S(2)}, u32[]{:S(2)}) %collective-permute-start.1) | collective-permute-done | bytes 278560 | tf_op jit(solution)/shard_map/ppermute | solution.py:327
  25.7 1.0 %shard_map.96 = (bf16[136,256]{1,0:T(8,128)(2,1)S(1)}, bf16[136,256]{1,0:T(8,128)(2,1)S(1)}, bf16[136,256]{1,0:T(8,128)(2,1)S(1)}, bf16[136,256]{1,0:T(8,128)(2,1)S(1)}) custom-call(s32[3]{0:T(128)S(1)} %pad_add_fusion.ids.refs_0_, bf16[136,1024]{1,0:T(8,128)(2,1)S(1)} %get-tuple-element.40.refs_0_.refs_4_, ...), custom_call_target="tpu_custom_call" | custom-call | flops 1392640 | bytes 1392640 | tf_op jit(solution)/shard_map/pallas_call | solution.py:312
  26.7 1.4 %collective-permute-start.15 = (bf16[3,136,1024]{2,1,0:T(8,128)(2,1)S(1)}, bf16[3,136,1024]{2,1,0:T(8,128)(2,1)S(1)}, u32[]{:S(2)}, u32[]{:S(2)}) collective-permute-start(bf16[3,136,1024]{2,1,0:T(8,128)(2,1)S(1)} %get-tuple-element.58), channel_id=1, source_target_pairs={{0,1},{2,3},{4,5},{6,7},{8,9},{10,11},{12,13},{14,15},{16,17},{18,... | collective-permute-start | bytes 2506760 | tf_op jit(solution)/shard_map/ppermute | solution.py:498
  28.2 1.3 %collective-permute-start.14 = (bf16[1,136,1024]{2,1,0:T(8,128)(2,1)S(1)}, bf16[1,136,1024]{2,1,0:T(8,128)(2,1)S(1)}, u32[]{:S(2)}, u32[]{:S(2)}) collective-permute-start(bf16[1,136,1024]{2,1,0:T(8,128)(2,1)S(1)} %get-tuple-element.57), channel_id=1, source_target_pairs={{0,1},{2,3},{4,5},{6,7},{8,9},{10,11},{12,13},{14,15},{16,17},{18,... | collective-permute-start | bytes 835592 | tf_op jit(solution)/shard_map/ppermute | solution.py:498
  29.5 1.5 %collective-permute-start.5 = (bf16[136,256]{1,0:T(8,128)(2,1)S(1)}, bf16[136,256]{1,0:T(8,128)(2,1)S(1)}, u32[]{:S(2)}, u32[]{:S(2)}) collective-permute-start(bf16[136,256]{1,0:T(8,128)(2,1)S(1)} %get-tuple-element.46), channel_id=1, source_target_pairs={{0,8},{1,9},{2,10},{3,11},{4,12},{5,13},{6,14},{7,15},{8,0},{9,1},... | collective-permute-start | bytes 208904 | tf_op jit(solution)/shard_map/ppermute | solution.py:327
  31.0 2.3 %collective-permute-start.6 = (bf16[136,256]{1,0:T(8,128)(2,1)S(1)}, bf16[136,256]{1,0:T(8,128)(2,1)S(1)}, u32[]{:S(2)}, u32[]{:S(2)}) collective-permute-start(bf16[136,256]{1,0:T(8,128)(2,1)S(1)} %get-tuple-element.47), channel_id=1, source_target_pairs={{0,16},{1,17},{2,18},{3,19},{4,20},{5,21},{6,22},{7,23},{8,24},{9,... | collective-permute-start | bytes 208904 | tf_op jit(solution)/shard_map/ppermute | solution.py:327
  33.3 0.0 collective-permute-start.7
  33.3 1.8 %collective-permute-start.8 = (f32[32]{0:T(128)S(1)}, f32[32]{0:T(128)S(1)}, u32[]{:S(2)}, u32[]{:S(2)}) collective-permute-start(f32[32]{0:T(128)S(1)} %copy-done.4), channel_id=1, source_target_pairs={{0,1},{1,0},{2,3},{3,2},{4,5},{5,4},{6,7},{7,6},{8,9},{9,8},{10,11... | collective-permute-start | bytes 392 | tf_op jit(solution)/shard_map/ppermute | solution.py:327
  35.1 0.7 collective-permute-done.6.refs_2_
  35.8 1.3 %collective-permute-start.9 = (f32[32]{0:T(128)S(1)}, f32[32]{0:T(128)S(1)}, u32[]{:S(2)}, u32[]{:S(2)}) collective-permute-start(f32[32]{0:T(128)S(1)} %copy-done.4), channel_id=1, source_target_pairs={{0,2},{1,3},{2,0},{3,1},{4,6},{5,7},{6,4},{7,5},{8,10},{9,11},{10,... | collective-permute-start | bytes 392 | tf_op jit(solution)/shard_map/ppermute | solution.py:327
  37.1 1.1 %collective-permute-done.7.refs_3_ = bf16[136,256]{1,0:T(8,128)(2,1)S(1)} collective-permute-done((bf16[136,256]{1,0:T(8,128)(2,1)S(1)}, bf16[136,256]{1,0:T(8,128)(2,1)S(1)}, u32[]{:S(2)}, u32[]{:S(2)}) %collective-permute-start.7) | collective-permute-done | bytes 69664 | tf_op jit(solution)/shard_map/ppermute | solution.py:327
  38.3 4.0 %collective-permute-start.10 = (f32[32]{0:T(128)S(1)}, f32[32]{0:T(128)S(1)}, u32[]{:S(2)}, u32[]{:S(2)}) collective-permute-start(f32[32]{0:T(128)S(1)} %copy-done.4), channel_id=1, source_target_pairs={{0,3},{1,2},{2,1},{3,0},{4,7},{5,6},{6,5},{7,4},{8,11},{9,10},{10,... | collective-permute-start | bytes 392 | tf_op jit(solution)/shard_map/ppermute | solution.py:327
  42.3 0.6 shard_map.97
  42.9 0.1 collective-permute-start.11
  43.0 2.0 %collective-permute-start.12 = (bf16[128,256]{1,0:T(8,128)(2,1)S(1)}, bf16[128,256]{1,0:T(8,128)(2,1)S(1)}, u32[]{:S(2)}, u32[]{:S(2)}) collective-permute-start(bf16[128,256]{1,0:T(8,128)(2,1)S(1)} %get-tuple-element.53), channel_id=1, source_target_pairs={{0,16},{1,17},{2,18},{3,19},{4,20},{5,21},{6,22},{7,23},{8,24},{9,... | collective-permute-start | bytes 196616 | tf_op jit(solution)/shard_map/ppermute | solution.py:327
  45.1 1.5 %collective-permute-start.13 = (bf16[128,256]{1,0:T(8,128)(2,1)S(1)}, bf16[128,256]{1,0:T(8,128)(2,1)S(1)}, u32[]{:S(2)}, u32[]{:S(2)}) collective-permute-start(bf16[128,256]{1,0:T(8,128)(2,1)S(1)} %get-tuple-element.54), channel_id=1, source_target_pairs={{0,24},{1,25},{2,26},{3,27},{4,28},{5,29},{6,30},{7,31},{8,16},{9,... | collective-permute-start | bytes 196616 | tf_op jit(solution)/shard_map/ppermute | solution.py:327
  46.6 1.9 %shard_map.98.refs_8_.refs_4_ = f32[8,256,1024]{2,1,0:T(8,128)S(1)} custom-call(s32[3]{0:T(128)S(1)} %pad_add_fusion.ids.refs_0_, bf16[256,8192]{1,0:T(8,128)(2,1)S(1)} %copy-done.2, bf16[128,256]{1,0:T(8,128)(2,1)S(1)} %get-tuple-element.49.refs_1_.refs_4_.refs_0_), custom_call_target="tpu_custom_call" | custom-call | flops 2008388608 | bytes 8388608 | tf_op jit(solution)/shard_map/pallas_call | solution.py:312
  48.5 0.8 %shard_map.99.refs_9_.refs_7_ = f32[8,8,1024]{2,1,0:T(8,128)S(1)} custom-call(s32[3]{0:T(128)S(1)} %pad_add_fusion.ids.refs_0_, f32[1,32]{1,0:T(1,128)S(1)} %bitcast.13, f32[1,32]{1,0:T(1,128)S(1)} %bitcast.14, f32[1,32]{1,0:T(1,128)S(1)} %bitcast.15, f32[1,32]{1,0:T(1,128)S(1)} %bitcast.16, bf16[128,256]{1,0:T(8,128)(2,1)S(1)} %get-tuple-element.49.refs_1_.refs_4_.refs_0_), custom_call_target="tpu_custom_call" | custom-call | flops 131328 | bytes 131328 | tf_op jit(solution)/shard_map/pallas_call | solution.py:312
  49.3 0.0 copy-start.3
  49.3 0.8 collective-permute-done.13.refs_3_
  50.1 1.1 %shard_map.100 = (bf16[128,1024]{1,0:T(8,128)(2,1)S(1)}, bf16[128,1024]{1,0:T(8,128)(2,1)S(1)}, bf16[128,1024]{1,0:T(8,128)(2,1)S(1)}, bf16[128,1024]{1,0:T(8,128)(2,1)S(1)}) custom-call(s32[3]{0:T(128)S(1)} %pad_add_fusion.ids.refs_0_, bf16[128,256]{1,0:T(8,128)(2,1)S(1)} %get-tuple-element.49.refs_1_.refs_4_.refs_0_, ...), custom_call_target="tpu_custom_call" | custom-call | flops 2424832 | bytes 2424832 | tf_op jit(solution)/shard_map/pallas_call | solution.py:312
  51.2 2.0 %collective-permute-start.20 = (bf16[128,1024]{1,0:T(8,128)(2,1)S(1)}, bf16[128,1024]{1,0:T(8,128)(2,1)S(1)}, u32[]{:S(2)}, u32[]{:S(2)}) collective-permute-start(bf16[128,1024]{1,0:T(8,128)(2,1)S(1)} %get-tuple-element.61), channel_id=1, source_target_pairs={{0,2},{1,3},{2,0},{3,1},{4,6},{5,7},{6,4},{7,5},{8,10},{9,11},{10,... | collective-permute-start | bytes 786440 | tf_op jit(solution)/shard_map/ppermute | solution.py:327
  53.3 1.2 %collective-permute-start.18 = (bf16[128,1024]{1,0:T(8,128)(2,1)S(1)}, bf16[128,1024]{1,0:T(8,128)(2,1)S(1)}, u32[]{:S(2)}, u32[]{:S(2)}) collective-permute-start(bf16[128,1024]{1,0:T(8,128)(2,1)S(1)} %get-tuple-element.60), channel_id=1, source_target_pairs={{0,4},{1,5},{2,6},{3,7},{4,0},{5,1},{6,2},{7,3},{8,12},{9,13},{10,... | collective-permute-start | bytes 786440 | tf_op jit(solution)/shard_map/ppermute | solution.py:327
  54.5 0.1 collective-permute-start.16
  54.5 1.9 %collective-permute-start.22 = (bf16[128,1024]{1,0:T(8,128)(2,1)S(1)}, bf16[128,1024]{1,0:T(8,128)(2,1)S(1)}, u32[]{:S(2)}, u32[]{:S(2)}) collective-permute-start(bf16[128,1024]{1,0:T(8,128)(2,1)S(1)} %get-tuple-element.62.refs_8_), channel_id=1, source_target_pairs={{0,1},{1,0},{2,3},{3,2},{4,5},{5,4},{6,7},{7,6},{8,9},{9,8},{10,11... | collective-permute-start | bytes 786440 | tf_op jit(solution)/shard_map/ppermute | solution.py:327
  56.4 2.1 %collective-permute-done.20.refs_9_ = bf16[128,1024]{1,0:T(8,128)(2,1)S(1)} collective-permute-done((bf16[128,1024]{1,0:T(8,128)(2,1)S(1)}, bf16[128,1024]{1,0:T(8,128)(2,1)S(1)}, u32[]{:S(2)}, u32[]{:S(2)}) %collective-permute-start.20) | collective-permute-done | bytes 262176 | tf_op jit(solution)/shard_map/ppermute | solution.py:327
  58.5 2.5 %collective-permute-start.21 = (bf16[128,1024]{1,0:T(8,128)(2,1)S(1)}, bf16[128,1024]{1,0:T(8,128)(2,1)S(1)}, u32[]{:S(2)}, u32[]{:S(2)}) collective-permute-start(bf16[128,1024]{1,0:T(8,128)(2,1)S(1)} %collective-permute-done.20.refs_9_), channel_id=1, source_target_pairs={{0,1},{1,0},{2,3},{3,2},{4,5},{5,4},{6,7},{7,6},{8,9},{9,8},{10,11... | collective-permute-start | bytes 786440 | tf_op jit(solution)/shard_map/ppermute | solution.py:327
  61.1 2.3 %collective-permute-start.19 = (bf16[128,1024]{1,0:T(8,128)(2,1)S(1)}, bf16[128,1024]{1,0:T(8,128)(2,1)S(1)}, u32[]{:S(2)}, u32[]{:S(2)}) collective-permute-start(bf16[128,1024]{1,0:T(8,128)(2,1)S(1)} %collective-permute-done.18.refs_9_), channel_id=1, source_target_pairs={{0,1},{1,0},{2,3},{3,2},{4,5},{5,4},{6,7},{7,6},{8,9},{9,8},{10,11... | collective-permute-start | bytes 786440 | tf_op jit(solution)/shard_map/ppermute | solution.py:327
  63.4 2.0 %shard_map.101.refs_12_ = bf16[256,8192]{1,0:T(8,128)(2,1)} custom-call(s32[3]{0:T(128)S(1)} %pad_add_fusion.ids.refs_0_, bf16[256,8192]{1,0:T(8,128)(2,1)S(1)} %copy-done, f32[8,256,1024]{2,1,0:T(8,128)S(1)} %get-tuple-element.38.refs_4_.refs_2_, f32[8,256,1024]{2,1,0:T(8,128)S(1)} %get-tuple-element.39.refs_3_, ...), custom_call_target="tpu_custom_call" | custom-call | flops 1000000000 | bytes 4194304 | tf_op jit(solution)/shard_map/pallas_call | solution.py:548
  65.4 2.0 %collective-permute-start.17 = (bf16[128,1024]{1,0:T(8,128)(2,1)S(1)}, bf16[128,1024]{1,0:T(8,128)(2,1)S(1)}, u32[]{:S(2)}, u32[]{:S(2)}) collective-permute-start(bf16[128,1024]{1,0:T(8,128)(2,1)S(1)} %collective-permute-done.16.refs_9_), channel_id=1, source_target_pairs={{0,1},{1,0},{2,3},{3,2},{4,5},{5,4},{6,7},{7,6},{8,9},{9,8},{10,11... | collective-permute-start | bytes 786440 | tf_op jit(solution)/shard_map/ppermute | solution.py:327
  67.4 2.7 %shard_map.102.refs_12_ = bf16[256,8192]{1,0:T(8,128)(2,1)} custom-call(s32[3]{0:T(128)S(1)} %pad_add_fusion.ids.refs_0_, bf16[256,8192]{1,0:T(8,128)(2,1)S(1)} %copy-done, f32[8,256,1024]{2,1,0:T(8,128)S(1)} %get-tuple-element.38.refs_4_.refs_2_, f32[8,256,1024]{2,1,0:T(8,128)S(1)} %get-tuple-element.39.refs_3_, ...), custom_call_target="tpu_custom_call", output_to_operand_aliasing={{}: (12, {})} | custom-call | flops 1000000000 | bytes 4194304 | tf_op jit(solution)/shard_map/pallas_call | solution.py:548
  70.1 2.9 %shard_map.103.refs_12_ = bf16[256,8192]{1,0:T(8,128)(2,1)} custom-call(s32[3]{0:T(128)S(1)} %pad_add_fusion.ids.refs_0_, bf16[256,8192]{1,0:T(8,128)(2,1)S(1)} %copy-done, f32[8,256,1024]{2,1,0:T(8,128)S(1)} %get-tuple-element.38.refs_4_.refs_2_, f32[8,256,1024]{2,1,0:T(8,128)S(1)} %get-tuple-element.39.refs_3_, ...), custom_call_target="tpu_custom_call", output_to_operand_aliasing={{}: (12, {})} | custom-call | flops 1000000000 | bytes 4194304 | tf_op jit(solution)/shard_map/pallas_call | solution.py:548
  73.1 2.8 %shard_map.104.refs_10_ = bf16[256,8192]{1,0:T(8,128)(2,1)} custom-call(s32[3]{0:T(128)S(1)} %pad_add_fusion.ids.refs_0_, bf16[256,8192]{1,0:T(8,128)(2,1)S(1)} %copy-done, f32[8,256,1024]{2,1,0:T(8,128)S(1)} %get-tuple-element.38.refs_4_.refs_2_, f32[8,256,1024]{2,1,0:T(8,128)S(1)} %get-tuple-element.39.refs_3_, ...), custom_call_target="tpu_custom_call", output_to_operand_aliasing={{}: (12, {})} | custom-call | flops 1000000000 | bytes 4194304 | tf_op jit(solution)/shard_map/pallas_call | solution.py:548
  75.9 2.0 %shard_map.105 = bf16[256,8192]{1,0:T(8,128)(2,1)} custom-call(s32[3]{0:T(128)S(1)} %pad_add_fusion.ids.refs_0_, bf16[256,8192]{1,0:T(8,128)(2,1)S(1)} %copy-done, f32[8,256,1024]{2,1,0:T(8,128)S(1)} %get-tuple-element.38.refs_4_.refs_2_, f32[8,256,1024]{2,1,0:T(8,128)S(1)} %get-tuple-element.39.refs_3_, ...), custom_call_target="tpu_custom_call", output_to_operand_aliasing={{}: (10, {})} | custom-call | flops 1000000000 | bytes 4194304 | tf_op jit(solution)/shard_map/pallas_call | solution.py:548
  (26 shorter events, 0.1 us)
Async XLA Ops:
  0.0 3.1 %copy-start.1 = (bf16[368,1024]{1,0:T(8,128)(2,1)S(1)}, bf16[368,1024]{1,0:T(8,128)(2,1)}, u32[]{:S(2)}) copy-start(bf16[368,1024]{1,0:T(8,128)(2,1)} %constant.17.clone.refs_4_.refs_6_) | copy-start | bytes 2260996
  0.0 3.1 %copy-start = (bf16[256,8192]{1,0:T(8,128)(2,1)S(1)}, bf16[256,8192]{1,0:T(8,128)(2,1)}, u32[]{:S(2)}) copy-start(bf16[256,8192]{1,0:T(8,128)(2,1)} %refs_1_.13) | copy-start | bytes 12582916
  5.2 7.4 %collective-permute-start = (bf16[3,136,1024]{2,1,0:T(8,128)(2,1)S(1)}, bf16[3,136,1024]{2,1,0:T(8,128)(2,1)S(1)}, u32[]{:S(2)}, u32[]{:S(2)}) collective-permute-start(bf16[3,136,1024]{2,1,0:T(8,128)(2,1)S(1)} %shard_map.93), channel_id=1, source_target_pairs={{0,1},{1,0},{2,3},{3,2},{4,5},{5,4},{6,7},{7,6},{8,9},{9,8},{10,11... | collective-permute-start | bytes 2506760 | tf_op jit(solution)/shard_map/ppermute | solution.py:327
  5.3 2.7 %collective-permute-start.3 = (bf16[1,136,1024]{2,1,0:T(8,128)(2,1)S(1)}, bf16[1,136,1024]{2,1,0:T(8,128)(2,1)S(1)}, u32[]{:S(2)}, u32[]{:S(2)}) collective-permute-start(bf16[1,136,1024]{2,1,0:T(8,128)(2,1)S(1)} %get-tuple-element.43), channel_id=1, source_target_pairs={{0,1},{1,0},{2,3},{3,2},{4,5},{5,4},{6,7},{7,6},{8,9},{9,8},{10,11... | collective-permute-start | bytes 835592 | tf_op jit(solution)/shard_map/ppermute | solution.py:327
  9.2 5.9 %copy-start.5 = (bf16[256,8,128]{2,1,0:T(8,128)(2,1)S(1)}, bf16[256,8,128]{2,1,0:T(8,128)(2,1)}, u32[]{:S(2)}) copy-start(bf16[256,8,128]{2,1,0:T(8,128)(2,1)} %refs_1_.8) | copy-start | bytes 1572868
  9.2 14.7 %collective-permute-start.4 = (bf16[136,1024]{1,0:T(8,128)(2,1)S(1)}, bf16[136,1024]{1,0:T(8,128)(2,1)S(1)}, u32[]{:S(2)}, u32[]{:S(2)}) collective-permute-start(bf16[136,1024]{1,0:T(8,128)(2,1)S(1)} %get-tuple-element.44), channel_id=1, source_target_pairs={{0,6},{1,7},{2,4},{3,5},{4,2},{5,3},{6,0},{7,1},{8,14},{9,15},{10,... | collective-permute-start | bytes 835592 | tf_op jit(solution)/shard_map/ppermute | solution.py:327
  14.8 10.9 %collective-permute-start.1 = (bf16[136,1024]{1,0:T(8,128)(2,1)S(1)}, bf16[136,1024]{1,0:T(8,128)(2,1)S(1)}, u32[]{:S(2)}, u32[]{:S(2)}) collective-permute-start(bf16[136,1024]{1,0:T(8,128)(2,1)S(1)} %get-tuple-element.41), channel_id=1, source_target_pairs={{0,2},{1,3},{2,0},{3,1},{4,6},{5,7},{6,4},{7,5},{8,10},{9,11},{10,... | collective-permute-start | bytes 835592 | tf_op jit(solution)/shard_map/ppermute | solution.py:327
  15.1 10.6 %collective-permute-start.2 = (bf16[136,1024]{1,0:T(8,128)(2,1)S(1)}, bf16[136,1024]{1,0:T(8,128)(2,1)S(1)}, u32[]{:S(2)}, u32[]{:S(2)}) collective-permute-start(bf16[136,1024]{1,0:T(8,128)(2,1)S(1)} %get-tuple-element.42), channel_id=1, source_target_pairs={{0,4},{1,5},{2,6},{3,7},{4,0},{5,1},{6,2},{7,3},{8,12},{9,13},{10,... | collective-permute-start | bytes 835592 | tf_op jit(solution)/shard_map/ppermute | solution.py:327
  25.7 7.6 %copy-start.4 = (f32[32]{0:T(128)S(1)}, f32[32]{0:T(128)}, u32[]{:S(2)}) copy-start(f32[32]{0:T(128)} %param.15) | copy-start | bytes 388
  25.7 20.9 %copy-start.2 = (bf16[256,8192]{1,0:T(8,128)(2,1)S(1)}, bf16[256,8192]{1,0:T(8,128)(2,1)}, u32[]{:S(2)}) copy-start(bf16[256,8192]{1,0:T(8,128)(2,1)} %refs_0_.11) | copy-start | bytes 12582916
  26.7 23.4 %collective-permute-start.15 = (bf16[3,136,1024]{2,1,0:T(8,128)(2,1)S(1)}, bf16[3,136,1024]{2,1,0:T(8,128)(2,1)S(1)}, u32[]{:S(2)}, u32[]{:S(2)}) collective-permute-start(bf16[3,136,1024]{2,1,0:T(8,128)(2,1)S(1)} %get-tuple-element.58), channel_id=1, source_target_pairs={{0,1},{2,3},{4,5},{6,7},{8,9},{10,11},{12,13},{14,15},{16,17},{18,... | collective-permute-start | bytes 2506760 | tf_op jit(solution)/shard_map/ppermute | solution.py:498
  28.2 21.9 %collective-permute-start.14 = (bf16[1,136,1024]{2,1,0:T(8,128)(2,1)S(1)}, bf16[1,136,1024]{2,1,0:T(8,128)(2,1)S(1)}, u32[]{:S(2)}, u32[]{:S(2)}) collective-permute-start(bf16[1,136,1024]{2,1,0:T(8,128)(2,1)S(1)} %get-tuple-element.57), channel_id=1, source_target_pairs={{0,1},{2,3},{4,5},{6,7},{8,9},{10,11},{12,13},{14,15},{16,17},{18,... | collective-permute-start | bytes 835592 | tf_op jit(solution)/shard_map/ppermute | solution.py:498
  29.5 3.9 %collective-permute-start.5 = (bf16[136,256]{1,0:T(8,128)(2,1)S(1)}, bf16[136,256]{1,0:T(8,128)(2,1)S(1)}, u32[]{:S(2)}, u32[]{:S(2)}) collective-permute-start(bf16[136,256]{1,0:T(8,128)(2,1)S(1)} %get-tuple-element.46), channel_id=1, source_target_pairs={{0,8},{1,9},{2,10},{3,11},{4,12},{5,13},{6,14},{7,15},{8,0},{9,1},... | collective-permute-start | bytes 208904 | tf_op jit(solution)/shard_map/ppermute | solution.py:327
  31.0 4.8 %collective-permute-start.6 = (bf16[136,256]{1,0:T(8,128)(2,1)S(1)}, bf16[136,256]{1,0:T(8,128)(2,1)S(1)}, u32[]{:S(2)}, u32[]{:S(2)}) collective-permute-start(bf16[136,256]{1,0:T(8,128)(2,1)S(1)} %get-tuple-element.47), channel_id=1, source_target_pairs={{0,16},{1,17},{2,18},{3,19},{4,20},{5,21},{6,22},{7,23},{8,24},{9,... | collective-permute-start | bytes 208904 | tf_op jit(solution)/shard_map/ppermute | solution.py:327
  33.3 5.0 %collective-permute-start.7 = (bf16[136,256]{1,0:T(8,128)(2,1)S(1)}, bf16[136,256]{1,0:T(8,128)(2,1)S(1)}, u32[]{:S(2)}, u32[]{:S(2)}) collective-permute-start(bf16[136,256]{1,0:T(8,128)(2,1)S(1)} %get-tuple-element.48), channel_id=1, source_target_pairs={{0,24},{1,25},{2,26},{3,27},{4,28},{5,29},{6,30},{7,31},{8,16},{9,... | collective-permute-start | bytes 208904 | tf_op jit(solution)/shard_map/ppermute | solution.py:327
  33.3 9.6 %collective-permute-start.8 = (f32[32]{0:T(128)S(1)}, f32[32]{0:T(128)S(1)}, u32[]{:S(2)}, u32[]{:S(2)}) collective-permute-start(f32[32]{0:T(128)S(1)} %copy-done.4), channel_id=1, source_target_pairs={{0,1},{1,0},{2,3},{3,2},{4,5},{5,4},{6,7},{7,6},{8,9},{9,8},{10,11... | collective-permute-start | bytes 392 | tf_op jit(solution)/shard_map/ppermute | solution.py:327
  35.8 7.2 %collective-permute-start.9 = (f32[32]{0:T(128)S(1)}, f32[32]{0:T(128)S(1)}, u32[]{:S(2)}, u32[]{:S(2)}) collective-permute-start(f32[32]{0:T(128)S(1)} %copy-done.4), channel_id=1, source_target_pairs={{0,2},{1,3},{2,0},{3,1},{4,6},{5,7},{6,4},{7,5},{8,10},{9,11},{10,... | collective-permute-start | bytes 392 | tf_op jit(solution)/shard_map/ppermute | solution.py:327
  38.3 6.8 %collective-permute-start.10 = (f32[32]{0:T(128)S(1)}, f32[32]{0:T(128)S(1)}, u32[]{:S(2)}, u32[]{:S(2)}) collective-permute-start(f32[32]{0:T(128)S(1)} %copy-done.4), channel_id=1, source_target_pairs={{0,3},{1,2},{2,1},{3,0},{4,7},{5,6},{6,5},{7,4},{8,11},{9,10},{10,... | collective-permute-start | bytes 392 | tf_op jit(solution)/shard_map/ppermute | solution.py:327
  42.9 6.4 %collective-permute-start.11 = (bf16[128,256]{1,0:T(8,128)(2,1)S(1)}, bf16[128,256]{1,0:T(8,128)(2,1)S(1)}, u32[]{:S(2)}, u32[]{:S(2)}) collective-permute-start(bf16[128,256]{1,0:T(8,128)(2,1)S(1)} %get-tuple-element.52), channel_id=1, source_target_pairs={{0,8},{1,9},{2,10},{3,11},{4,12},{5,13},{6,14},{7,15},{8,0},{9,1},... | collective-permute-start | bytes 196616 | tf_op jit(solution)/shard_map/ppermute | solution.py:327
  43.0 6.3 %collective-permute-start.12 = (bf16[128,256]{1,0:T(8,128)(2,1)S(1)}, bf16[128,256]{1,0:T(8,128)(2,1)S(1)}, u32[]{:S(2)}, u32[]{:S(2)}) collective-permute-start(bf16[128,256]{1,0:T(8,128)(2,1)S(1)} %get-tuple-element.53), channel_id=1, source_target_pairs={{0,16},{1,17},{2,18},{3,19},{4,20},{5,21},{6,22},{7,23},{8,24},{9,... | collective-permute-start | bytes 196616 | tf_op jit(solution)/shard_map/ppermute | solution.py:327
  45.1 5.0 %collective-permute-start.13 = (bf16[128,256]{1,0:T(8,128)(2,1)S(1)}, bf16[128,256]{1,0:T(8,128)(2,1)S(1)}, u32[]{:S(2)}, u32[]{:S(2)}) collective-permute-start(bf16[128,256]{1,0:T(8,128)(2,1)S(1)} %get-tuple-element.54), channel_id=1, source_target_pairs={{0,24},{1,25},{2,26},{3,27},{4,28},{5,29},{6,30},{7,31},{8,16},{9,... | collective-permute-start | bytes 196616 | tf_op jit(solution)/shard_map/ppermute | solution.py:327
  49.3 14.1 %copy-start.3 = (f32[8192]{0:T(1024)S(1)}, f32[8192]{0:T(1024)}, u32[]{:S(2)}) copy-start(f32[8192]{0:T(1024)} %param.16) | copy-start | bytes 98308
  51.2 7.3 %collective-permute-start.20 = (bf16[128,1024]{1,0:T(8,128)(2,1)S(1)}, bf16[128,1024]{1,0:T(8,128)(2,1)S(1)}, u32[]{:S(2)}, u32[]{:S(2)}) collective-permute-start(bf16[128,1024]{1,0:T(8,128)(2,1)S(1)} %get-tuple-element.61), channel_id=1, source_target_pairs={{0,2},{1,3},{2,0},{3,1},{4,6},{5,7},{6,4},{7,5},{8,10},{9,11},{10,... | collective-permute-start | bytes 786440 | tf_op jit(solution)/shard_map/ppermute | solution.py:327
  53.3 7.8 %collective-permute-start.18 = (bf16[128,1024]{1,0:T(8,128)(2,1)S(1)}, bf16[128,1024]{1,0:T(8,128)(2,1)S(1)}, u32[]{:S(2)}, u32[]{:S(2)}) collective-permute-start(bf16[128,1024]{1,0:T(8,128)(2,1)S(1)} %get-tuple-element.60), channel_id=1, source_target_pairs={{0,4},{1,5},{2,6},{3,7},{4,0},{5,1},{6,2},{7,3},{8,12},{9,13},{10,... | collective-permute-start | bytes 786440 | tf_op jit(solution)/shard_map/ppermute | solution.py:327
  54.5 10.9 %collective-permute-start.16 = (bf16[128,1024]{1,0:T(8,128)(2,1)S(1)}, bf16[128,1024]{1,0:T(8,128)(2,1)S(1)}, u32[]{:S(2)}, u32[]{:S(2)}) collective-permute-start(bf16[128,1024]{1,0:T(8,128)(2,1)S(1)} %get-tuple-element.59), channel_id=1, source_target_pairs={{0,6},{1,7},{2,4},{3,5},{4,2},{5,3},{6,0},{7,1},{8,14},{9,15},{10,... | collective-permute-start | bytes 786440 | tf_op jit(solution)/shard_map/ppermute | solution.py:327
  54.5 12.9 %collective-permute-start.22 = (bf16[128,1024]{1,0:T(8,128)(2,1)S(1)}, bf16[128,1024]{1,0:T(8,128)(2,1)S(1)}, u32[]{:S(2)}, u32[]{:S(2)}) collective-permute-start(bf16[128,1024]{1,0:T(8,128)(2,1)S(1)} %get-tuple-element.62.refs_8_), channel_id=1, source_target_pairs={{0,1},{1,0},{2,3},{3,2},{4,5},{5,4},{6,7},{7,6},{8,9},{9,8},{10,11... | collective-permute-start | bytes 786440 | tf_op jit(solution)/shard_map/ppermute | solution.py:327
  58.5 11.6 %collective-permute-start.21 = (bf16[128,1024]{1,0:T(8,128)(2,1)S(1)}, bf16[128,1024]{1,0:T(8,128)(2,1)S(1)}, u32[]{:S(2)}, u32[]{:S(2)}) collective-permute-start(bf16[128,1024]{1,0:T(8,128)(2,1)S(1)} %collective-permute-done.20.refs_9_), channel_id=1, source_target_pairs={{0,1},{1,0},{2,3},{3,2},{4,5},{5,4},{6,7},{7,6},{8,9},{9,8},{10,11... | collective-permute-start | bytes 786440 | tf_op jit(solution)/shard_map/ppermute | solution.py:327
  61.1 12.0 %collective-permute-start.19 = (bf16[128,1024]{1,0:T(8,128)(2,1)S(1)}, bf16[128,1024]{1,0:T(8,128)(2,1)S(1)}, u32[]{:S(2)}, u32[]{:S(2)}) collective-permute-start(bf16[128,1024]{1,0:T(8,128)(2,1)S(1)} %collective-permute-done.18.refs_9_), channel_id=1, source_target_pairs={{0,1},{1,0},{2,3},{3,2},{4,5},{5,4},{6,7},{7,6},{8,9},{9,8},{10,11... | collective-permute-start | bytes 786440 | tf_op jit(solution)/shard_map/ppermute | solution.py:327
  65.4 10.5 %collective-permute-start.17 = (bf16[128,1024]{1,0:T(8,128)(2,1)S(1)}, bf16[128,1024]{1,0:T(8,128)(2,1)S(1)}, u32[]{:S(2)}, u32[]{:S(2)}) collective-permute-start(bf16[128,1024]{1,0:T(8,128)(2,1)S(1)} %collective-permute-done.16.refs_9_), channel_id=1, source_target_pairs={{0,1},{1,0},{2,3},{3,2},{4,5},{5,4},{6,7},{7,6},{8,9},{9,8},{10,11... | collective-permute-start | bytes 786440 | tf_op jit(solution)/shard_map/ppermute | solution.py:327
